TPU v7x, 32 devices: a whole 2x2x4 slice. The times are simulated.
32 devices in a mesh: dp: 4 (over z), fsdp: 8 (over y, x, core).
Axes of the slice: x: 2, y: 2, z: 4, core: 2. Of those that a mesh axis runs over, the one named last changes fastest.
Arguments:
- tokens: bfloat16 [4096, 2048], P(('dp', 'fsdp')), may hold values from -6 to 6
- ln_gain: float32 [2048], replicated, may hold values from 0.5 to 1.5
- ln_shift: float32 [2048], replicated, may hold values from -3 to 3
- w_qkv: bfloat16 [2048, 6144], P(('dp', 'fsdp')), may hold values from -0.125 to 0.125
- b_qkv: float32 [6144], replicated, may hold values from -3 to 3
- w_out: bfloat16 [2048, 2048], P(('dp', 'fsdp')), may hold values from -0.5 to 0.5
- w_gate: bfloat16 [2048, 5632], P(('dp', 'fsdp')), may hold values from -0.125 to 0.125
- w_up: bfloat16 [2048, 5632], P(('dp', 'fsdp')), may hold values from -0.125 to 0.125
- w_down: bfloat16 [5632, 2048], P(('dp', 'fsdp')), may hold values from -0.078125 to 0.078125
- grad_out: bfloat16 [4096, 2048], P(('dp', 'fsdp')), may hold values from -6 to 6
- seq_lengths: int32 [32, 4], P(('dp', 'fsdp')), may hold values from 0 to 128, as said below
Outputs:
- output: bfloat16 [4096, 2048], P(('dp', 'fsdp'))
- grad_tokens: bfloat16 [4096, 2048], P(('dp', 'fsdp'))
- grad_w_qkv: float32 [2048, 6144], P(('dp', 'fsdp'))
- grad_w_out: float32 [2048, 2048], P(('dp', 'fsdp'))
- grad_w_gate: float32 [2048, 5632], P(('dp', 'fsdp'))
- grad_w_up: float32 [2048, 5632], P(('dp', 'fsdp'))
- grad_w_down: float32 [5632, 2048], P(('dp', 'fsdp'))
- grad_gain: float32 [2048], P(('dp', 'fsdp'))
- grad_shift: float32 [2048], P(('dp', 'fsdp'))
- grad_bias: float32 [6144], P(('dp', 'fsdp'))
Inputs may be any that keep to these rules, and one draw needn't show every extreme that they name: `seq_lengths`: each device's row of lengths sums to at most 128; some device holds a single sequence of exactly 128 tokens, and some slots are empty (length 0).
All inputs are finite; a program needn't handle non-finite values.
Results may differ from a plain program's by a relative error of at most 0.012.
Values may be sent and summed in bfloat16 or wider, within the bound.
No kernel may reach another device: no remote copies, remote signals or barrier semaphores. Data moves between devices by JAX's collectives and lax.ppermute only.
A program may use at most 256 MiB of HBM per device.

v0:
```python
import math

import jax
import jax.numpy as jnp
from jax import lax
from jax.sharding import PartitionSpec as P

HD = 64
ROT = 16


EPS = 1e-05
NEG = -1e30
CONTRACT_ROWS = (((0,), (0,)), ((), ()))
CONTRACT_COLS = (((1,), (1,)), ((), ()))


def block_terms(lengths_row, rows_tok):
    ends = jnp.cumsum(lengths_row)
    place = jnp.arange(rows_tok, dtype=jnp.int32)
    segment = jnp.sum((place[:, None] >= ends[None, :]).astype(jnp.int32), axis=1)
    starts = jnp.concatenate([ends - lengths_row, ends[-1:]])
    labels = jnp.arange(starts.shape[0], dtype=jnp.int32)
    begin = jnp.sum(jnp.where(segment[:, None] == labels[None, :], starts[None, :], 0), axis=1)
    position = (place - begin).astype(jnp.float32)
    valid = segment < lengths_row.shape[0]
    label_tok = jnp.where(valid, segment, lengths_row.shape[0] + place)
    allowed = (label_tok[:, None] == label_tok[None, :]) & (place[None, :] <= place[:, None])
    return (position, valid, allowed)


def angles(position):
    half = ROT // 2
    freq = jnp.exp(jnp.arange(half, dtype=jnp.float32) * (-2.0 * math.log(10000.0) / ROT))
    turn = position[:, None] * freq[None, :]
    return (jnp.cos(turn), jnp.sin(turn))


def rotate(heads_in, cosine, sine):
    half = ROT // 2
    first = heads_in[..., :half]
    second = heads_in[..., half:ROT]
    cos_b = cosine[:, None, :]
    sin_b = sine[:, None, :]
    return jnp.concatenate(
        [first * cos_b - second * sin_b, second * cos_b + first * sin_b, heads_in[..., ROT:]],
        axis=-1,
    )


def alternate(first, second, shards):
    rows_tok = first.shape[0]
    joined = jnp.concatenate(
        [first.reshape(rows_tok, shards, -1), second.reshape(rows_tok, shards, -1)], axis=2
    )
    return joined.reshape(rows_tok, -1)


def separate(joined, shards, split_at):
    rows_tok = joined.shape[0]
    blocks = joined.reshape(rows_tok, shards, -1)
    return (
        blocks[:, :, :split_at].reshape(rows_tok, -1),
        blocks[:, :, split_at:].reshape(rows_tok, -1),
    )


def on_device(
    tokens, ln_gain, ln_shift, w_qkv, b_qkv, w_out, w_gate, w_up, w_down, grad_out, seq_lengths
):
    shards = lax.axis_size(("dp", "fsdp"))
    rows_tok, width = tokens.shape
    heads = width // HD
    inner = w_gate.shape[1]
    own_rows = w_qkv.shape[0]
    position, valid, allowed = block_terms(seq_lengths[0], rows_tok)
    cosine, sine = angles(position)
    keep_row = valid.astype(jnp.float32)[:, None]
    widened = tokens.astype(jnp.float32)
    centered = widened - jnp.mean(widened, axis=1, keepdims=True)
    inv_std = lax.rsqrt(jnp.mean(centered * centered, axis=1, keepdims=True) + EPS)
    scaled = centered * inv_std
    normed = (scaled * ln_gain + ln_shift).astype(jnp.bfloat16)
    mixer = jnp.concatenate([w_out, w_down], axis=0)
    pieces = (
        lax.all_gather(w_qkv, ("dp", "fsdp"), axis=0, tiled=True),
        lax.all_gather(w_gate, ("dp", "fsdp"), axis=0, tiled=True),
        lax.all_gather(w_up, ("dp", "fsdp"), axis=0, tiled=True),
    )
    columns = normed
    proj_qkv, proj_gate, proj_up = tuple(
        (jnp.dot(columns, piece, preferred_element_type=jnp.float32) for piece in pieces)
    )
    split_qkv = (proj_qkv + b_qkv).reshape(rows_tok, 3, heads, HD)
    query = rotate(split_qkv[:, 0], cosine, sine).astype(jnp.bfloat16)
    keys = rotate(split_qkv[:, 1], cosine, sine).astype(jnp.bfloat16)
    values = split_qkv[:, 2].astype(jnp.bfloat16)
    scores = jnp.einsum("qhd,khd->hqk", query, keys, preferred_element_type=jnp.float32) * 0.125
    scores = jnp.where(allowed[None], scores, NEG)
    peak = jnp.max(scores, axis=2, keepdims=True)
    lifted = jnp.exp(scores - peak)
    row_total = jnp.sum(lifted, axis=2, keepdims=True)
    probs = lifted / row_total
    log_total = peak + jnp.log(row_total)
    attended = jnp.einsum(
        "hqk,khd->qhd", probs.astype(jnp.bfloat16), values, preferred_element_type=jnp.float32
    )
    attended = attended.reshape(rows_tok, width).astype(jnp.bfloat16)
    sigma = jax.nn.sigmoid(proj_gate)
    activ = proj_gate * sigma
    hidden = (activ * proj_up).astype(jnp.bfloat16)
    joined = alternate(attended, hidden, shards)
    columns = joined
    branch_sum = jnp.dot(
        columns,
        lax.all_gather(mixer, ("dp", "fsdp"), axis=0, tiled=True),
        preferred_element_type=jnp.float32,
    )
    output = (widened + keep_row * branch_sum).astype(jnp.bfloat16)
    masked = (grad_out.astype(jnp.float32) * keep_row).astype(jnp.bfloat16)
    back_mix = lax.dot_general(
        masked,
        lax.all_gather(mixer, ("dp", "fsdp"), axis=0, tiled=True),
        CONTRACT_COLS,
        preferred_element_type=jnp.float32,
    )
    grad_att, grad_hid = separate(back_mix, shards, own_rows)
    grad_mixed = grad_att.astype(jnp.bfloat16).reshape(rows_tok, heads, HD)
    redo = jnp.einsum("qhd,khd->hqk", query, keys, preferred_element_type=jnp.float32) * 0.125
    redo = jnp.where(allowed[None], redo, NEG)
    probs_again = jnp.exp(redo - log_total)
    grad_probs = jnp.einsum("qhd,khd->hqk", grad_mixed, values, preferred_element_type=jnp.float32)
    inner_sum = jnp.sum(probs_again * grad_probs, axis=2, keepdims=True)
    grad_scores = (probs_again * (grad_probs - inner_sum)).astype(jnp.bfloat16)
    grad_query = (
        jnp.einsum("hqk,khd->qhd", grad_scores, keys, preferred_element_type=jnp.float32) * 0.125
    )
    grad_keys = (
        jnp.einsum("hqk,qhd->khd", grad_scores, query, preferred_element_type=jnp.float32) * 0.125
    )
    grad_values = jnp.einsum(
        "hqk,qhd->khd",
        probs_again.astype(jnp.bfloat16),
        grad_mixed,
        preferred_element_type=jnp.float32,
    )
    grad_proj = jnp.stack(
        [rotate(grad_query, cosine, -sine), rotate(grad_keys, cosine, -sine), grad_values], axis=1
    )
    grad_proj = grad_proj.reshape(rows_tok, 3 * width).astype(jnp.bfloat16)
    slope = sigma * (1.0 + proj_gate * (1.0 - sigma))
    grad_gate = (grad_hid * proj_up * slope).astype(jnp.bfloat16)
    grad_up = (grad_hid * activ).astype(jnp.bfloat16)
    pieces = lax.all_gather((w_qkv, w_gate, w_up), ("dp", "fsdp"), axis=0, tiled=True)
    first = lax.dot_general(grad_proj, pieces[0], CONTRACT_COLS, preferred_element_type=jnp.float32)
    second = lax.dot_general(
        grad_gate, pieces[1], CONTRACT_COLS, preferred_element_type=jnp.float32
    )
    third = lax.dot_general(grad_up, pieces[2], CONTRACT_COLS, preferred_element_type=jnp.float32)
    grad_norm = first + second + third
    gain_part = jnp.sum(grad_norm * scaled, axis=0)
    shift_part = jnp.sum(grad_norm, axis=0)
    bias_part = jnp.sum(grad_proj.astype(jnp.float32), axis=0).reshape(width, 3)
    lifted_grad = grad_norm * ln_gain
    grad_in = inv_std * (
        lifted_grad
        - jnp.mean(lifted_grad, axis=1, keepdims=True)
        - scaled * jnp.mean(lifted_grad * scaled, axis=1, keepdims=True)
    )
    grad_tokens = (grad_out.astype(jnp.float32) + grad_in).astype(jnp.bfloat16)
    stats = jnp.concatenate(
        [gain_part[:, None], shift_part[:, None], bias_part, jnp.zeros((width, 123), jnp.float32)],
        axis=1,
    )
    outer = lax.axis_size("fsdp")
    group_rows = own_rows * outer
    normed_cols, joined_cols = (
        lax.all_to_all(normed, "dp", split_axis=1, concat_axis=0, tiled=True),
        lax.all_to_all(joined, "dp", split_axis=1, concat_axis=0, tiled=True),
    )
    stat_parts = lax.all_to_all(jnp.transpose(stats), "dp", split_axis=1, concat_axis=0, tiled=True)
    stat_sum = jnp.transpose(jnp.sum(stat_parts.reshape(-1, stats.shape[1], group_rows), axis=0))
    pieces = (
        lax.all_gather(grad_proj, "dp", axis=0, tiled=True),
        lax.all_gather(grad_gate, "dp", axis=0, tiled=True),
        lax.all_gather(grad_up, "dp", axis=0, tiled=True),
        lax.all_gather(masked, "dp", axis=0, tiled=True),
    )
    blocks = [
        lax.dot_general(normed_cols, piece, CONTRACT_ROWS, preferred_element_type=jnp.float32)
        for piece in pieces[:3]
    ]
    mixed_part = lax.dot_general(
        joined_cols, pieces[3], CONTRACT_ROWS, preferred_element_type=jnp.float32
    )
    input_part = jnp.concatenate(blocks, axis=1)
    input_part = jnp.concatenate([input_part, stat_sum], axis=1)
    input_sum, mixer_sum = (
        lax.psum_scatter(
            input_part.astype(jnp.bfloat16), "fsdp", scatter_dimension=0, tiled=True
        ).astype(jnp.float32),
        lax.psum_scatter(
            mixed_part.astype(jnp.bfloat16), "fsdp", scatter_dimension=0, tiled=True
        ).astype(jnp.float32),
    )
    qkv_cols = 3 * width
    grad_w_qkv = input_sum[:, :qkv_cols]
    grad_w_gate = input_sum[:, qkv_cols : qkv_cols + inner]
    grad_w_up = input_sum[:, qkv_cols + inner : qkv_cols + 2 * inner]
    tail_cols = input_sum[:, qkv_cols + 2 * inner :]
    grad_gain = tail_cols[:, 0]
    grad_shift = tail_cols[:, 1]
    grad_bias = tail_cols[:, 2:5].reshape(-1)
    grad_w_out = mixer_sum[:own_rows]
    grad_w_down = mixer_sum[own_rows:]
    return (
        output,
        grad_tokens,
        grad_w_qkv,
        grad_w_out,
        grad_w_gate,
        grad_w_up,
        grad_w_down,
        grad_gain,
        grad_shift,
        grad_bias,
    )


def solution(mesh):
    placed = (
        P(("dp", "fsdp"), None),
        P(),
        P(),
        P(("dp", "fsdp"), None),
        P(),
        P(("dp", "fsdp"), None),
        P(("dp", "fsdp"), None),
        P(("dp", "fsdp"), None),
        P(("dp", "fsdp"), None),
        P(("dp", "fsdp"), None),
        P(("dp", "fsdp"), None),
    )
    return jax.shard_map(
        on_device,
        mesh=mesh,
        in_specs=placed,
        out_specs=(
            P(("dp", "fsdp"), None),
            P(("dp", "fsdp"), None),
            P(("dp", "fsdp"), None),
            P(("dp", "fsdp"), None),
            P(("dp", "fsdp"), None),
            P(("dp", "fsdp"), None),
            P(("dp", "fsdp"), None),
            P(("dp", "fsdp")),
            P(("dp", "fsdp")),
            P(("dp", "fsdp")),
        ),
        check_vma=False,
    )
```

profile of v0, /device:TPU:0, one launch (start us, length us, event | category | flops | bytes accessed | tf_op | source)
XLA Modules:
  0.0 1286.7 jit_solution(11946301939778246751)
XLA Ops:
  13.9 144.3 %all-gather.13.cloned.1.call-done = bf16[2048,5632]{1,0:T(8,128)(2,1)} async-done(((bf16[64,5632]{1,0:T(8,128)(2,1)}), bf16[2048,5632]{1,0:T(8,128)(2,1)}) %all-gather.13.cloned.1.call-update) | async-done | bytes 23068688 | tf_op jit(solution)/shard_map/all_gather | solution.py:88
  158.2 12.3 fusion.36
  170.5 174.2 %all-gather.15.cloned.1.call-done = bf16[7680,2048]{1,0:T(8,128)(2,1)} async-done(((bf16[240,2048]{1,0:T(8,128)(2,1)}), bf16[7680,2048]{1,0:T(8,128)(2,1)}) %all-gather.15.cloned.1.call-update) | async-done | bytes 31457296 | tf_op jit(solution)/shard_map/all_gather | solution.py:116
  344.7 14.4 %fusion.37 = f32[128,7680]{0,1:T(8,128)S(1)} fusion(bf16[128,2048]{1,0:T(8,128)(2,1)S(1)} %copy-done.8, bf16[7680,2048]{1,0:T(8,128)(2,1)} %all-gather.15.cloned.1.call-done), kind=kOutput, calls=%fused_computation.107 | convolution fusion | flops 4026531840 | bytes 35913728 | tf_op jit(solution)/shard_map/dot_general | solution.py:121
  365.3 125.1 %all-gather.11.cloned.1.call-done = bf16[2048,5632]{1,0:T(8,128)(2,1)} async-done(((bf16[64,5632]{1,0:T(8,128)(2,1)}), bf16[2048,5632]{1,0:T(8,128)(2,1)}) %all-gather.11.cloned.1.call-update) | async-done | bytes 23068688 | tf_op jit(solution)/shard_map/all_gather | solution.py:87
  490.4 15.8 %multiply_convert_fusion = (bf16[128,5632]{1,0:T(8,128)(2,1)}, bf16[128,5632]{1,0:T(8,128)(2,1)}, bf16[128,5632]{1,0:T(8,128)(2,1)}) fusion(f32[128,5632]{1,0:T(8,128)} %copy.50, f32[128,5632]{1,0:T(8,128)} %fusion.36, bf16[128,2048]{1,0:T(8,128)(2,1)S(1)} %fusion.15, bf16[2048,5632]{1,0:T(8,128)(2,1)} %all-gather.11.cloned.1.call-done), kind=kOutput, calls=%fused_computation.8 | convolution fusion | flops 2963603456 | bytes 33685504 | tf_op jit(solution)/shard_map/dot_general | solution.py:92
  508.9 137.1 %all-gather.9.cloned.1.call-done = bf16[2048,6144]{1,0:T(8,128)(2,1)} async-done(((bf16[64,6144]{1,0:T(8,128)(2,1)}), bf16[2048,6144]{1,0:T(8,128)(2,1)}) %all-gather.9.cloned.1.call-update) | async-done | bytes 25165840 | tf_op jit(solution)/shard_map/all_gather | solution.py:86
  645.9 13.5 %convolution_add_fusion = f32[128,6144]{1,0:T(8,128)} fusion(bf16[128,2048]{1,0:T(8,128)(2,1)S(1)} %fusion.15, bf16[2048,6144]{1,0:T(8,128)(2,1)} %all-gather.9.cloned.1.call-done, f32[6144]{0:T(1024)S(1)} %copy-done.15), kind=kOutput, calls=%fused_computation.5 | convolution fusion | flops 3222011904 | bytes 28860416 | tf_op jit(solution)/shard_map/dot_general | solution.py:92
  684.0 83.2 %all-to-all-done.2 = bf16[128,4,1920]{0,2,1:T(8,128)(2,1)S(1)} async-done(((bf16[128,4,1920]{0,2,1:T(8,128)(2,1)}), bf16[128,4,1920]{0,2,1:T(8,128)(2,1)S(1)}, u32[]{:S(2)}, u32[]{:S(2)}) %all-to-all-start.2) | async-done | bytes 1966112 | tf_op jit(solution)/shard_map/all_to_all | solution.py:179
  769.6 9.7 convolution_convert_fusion.3
  780.7 14.2 %fusion.38 = f32[128,2048]{1,0:T(8,128)} fusion(bf16[128,6144]{0,1:T(8,128)(2,1)S(1)} %bitcast.81, bf16[2048,6144]{1,0:T(8,128)(2,1)} %all-gather.9.cloned.1.call-done), kind=kOutput, calls=%fused_computation.108 | convolution fusion | flops 3221225472 | bytes 27787264 | tf_op jit(solution)/shard_map/dot_general | solution.py:155
  794.8 12.5 convolution_add_fusion.2
  807.3 13.6 %fusion.19 = (f32[2048]{0:T(1024)S(1)}, f32[128]{0:T(128)S(1)}, f32[128]{0:T(128)S(1)}, f32[2048]{0:T(1024)S(1)}, f32[128,2048]{1,0:T(8,128)}) fusion(bf16[128,2048]{1,0:T(8,128)(2,1)S(1)} %copy-done.6, f32[128]{0:T(128)S(1)} %add_rsqrt_fusion, f32[128]{0:T(128)S(1)} %broadcast_multiply_fusion.2, f32[2048]{0:T(1024)S(1)} %copy-done.14, ...), kind=kOutput, calls=%fused_computation.49 | convolution fusion | flops 2955669504 | bytes 27158528 | tf_op jit(solution)/shard_map/dot_general | solution.py:159
  830.9 50.8 %all-to-all-done.1 = f32[128,4,512]{0,2,1:T(8,128)S(1)} async-done(((f32[128,4,512]{0,2,1:T(8,128)}), f32[128,4,512]{0,2,1:T(8,128)S(1)}, u32[]{:S(2)}, u32[]{:S(2)}) %all-to-all-start.1) | async-done | bytes 1048608 | tf_op jit(solution)/shard_map/all_to_all | solution.py:181
  885.3 26.9 %all-to-all-done = bf16[128,4,512]{2,0,1:T(8,128)(2,1)S(1)} async-done(((bf16[128,4,512]{2,0,1:T(8,128)(2,1)}), bf16[128,4,512]{2,0,1:T(8,128)(2,1)S(1)}, u32[]{:S(2)}, u32[]{:S(2)}) %all-to-all-start) | async-done | bytes 524320 | tf_op jit(solution)/shard_map/all_to_all | solution.py:178
  912.2 7.7 convolution_convert_fusion
  919.9 40.7 %all-gather.19.cloned.1.call-done = bf16[512,5632]{1,0:T(8,128)(2,1)} async-done(((bf16[128,5632]{1,0:T(8,128)(2,1)}), bf16[512,5632]{1,0:T(8,128)(2,1)}) %all-gather.19.cloned.1.call-update) | async-done | bytes 5767184 | tf_op jit(solution)/shard_map/all_gather | solution.py:185
  960.6 7.6 convolution_convert_fusion.1
  968.2 108.2 %all-gather.17.cloned.1.call-done = bf16[512,6144]{0,1:T(8,128)(2,1)} async-done(((bf16[128,6144]{0,1:T(8,128)(2,1)}), bf16[512,6144]{0,1:T(8,128)(2,1)}) %all-gather.17.cloned.1.call-update) | async-done | bytes 6291472 | tf_op jit(solution)/shard_map/all_gather | solution.py:184
  1076.4 8.4 convolution_convert_fusion.2
  1084.8 10.9 pad_maximum_fusion
  1098.4 16.9 %fusion.2 = bf16[128,2048]{1,0:T(8,128)(2,1)} fusion(bf16[128,7680]{0,1:T(8,128)(2,1)} %bitcast.10, bf16[7680,2048]{1,0:T(8,128)(2,1)} %all-gather.15.cloned.1.call-done, bf16[128,2048]{1,0:T(8,128)(2,1)S(1)} %copy-done.6, f32[128]{0:T(128)S(1)} %compare_convert_fusion), kind=kOutput, calls=%fused_computation.17 | convolution fusion | flops 4027580416 | bytes 34472448 | tf_op jit(solution)/shard_map/dot_general | solution.py:114
  1115.2 32.3 %reduce-scatter.5.cloned.1.call-done = bf16[240,2048]{1,0:T(8,128)(2,1)} async-done(((bf16[1920,2048]{1,0:T(8,128)(2,1)}), bf16[240,2048]{1,0:T(8,128)(2,1)}) %reduce-scatter.5.cloned.1.call-update) | async-done | bytes 983056 | tf_op jit(solution)/shard_map/reduce_scatter | solution.py:202
  1150.8 122.3 %reduce-scatter.3.cloned.1.call-done = bf16[64,17536]{1,0:T(8,128)(2,1)} async-done(((bf16[512,17536]{1,0:T(8,128)(2,1)}), bf16[64,17536]{1,0:T(8,128)(2,1)}) %reduce-scatter.3.cloned.1.call-update) | async-done | bytes 2244624 | tf_op jit(solution)/shard_map/reduce_scatter | solution.py:199
  (123 shorter events, 69.6 us)
Async XLA Ops:
  7.2 4.5 copy-start.17
  7.2 4.7 copy-start.11
  7.2 151.0 %all-gather.13.cloned.1.call-start = ((), (), s32[]{:S(2)}) async-start(), calls=%async_computation.7 | async-start | bytes 23789568 | tf_op jit(solution)/shard_map/all_gather | solution.py:88
  7.9 5.0 copy-start.6
  7.9 336.8 %all-gather.15.cloned.1.call-start = ((), (), s32[]{:S(2)}) async-start(), calls=%async_computation.8 | async-start | bytes 32440320 | tf_op jit(solution)/shard_map/all_gather | solution.py:116
  10.3 3.2 copy-start.14
  10.3 3.2 copy-start.16
  10.3 480.1 %all-gather.11.cloned.1.call-start = ((), (), s32[]{:S(2)}) async-start(), calls=%async_computation.6 | async-start | bytes 23789568 | tf_op jit(solution)/shard_map/all_gather | solution.py:87
  11.0 634.9 %all-gather.9.cloned.1.call-start = ((), (), s32[]{:S(2)}) async-start(), calls=%async_computation.5 | async-start | bytes 25952256 | tf_op jit(solution)/shard_map/all_gather | solution.py:86
  11.6 758.0 %all-gather.23.cloned.1.call-start = ((), (), s32[]{:S(2)}) async-start(), calls=%async_computation.13 | async-start | bytes 2621440 | tf_op jit(solution)/shard_map/all_gather | solution.py:187
  12.9 899.3 %all-gather.21.cloned.1.call-start = ((), (), s32[]{:S(2)}) async-start(), calls=%async_computation.11 | async-start | bytes 7208960 | tf_op jit(solution)/shard_map/all_gather | solution.py:186
  13.9 330.9 %copy-start.8 = (bf16[128,2048]{1,0:T(8,128)(2,1)S(1)}, bf16[128,2048]{1,0:T(8,128)(2,1)}, u32[]{:S(2)}) copy-start(bf16[128,2048]{1,0:T(8,128)(2,1)} %fusion.21) | copy-start | bytes 1572868
  506.2 139.7 %copy-start.15 = (f32[6144]{0:T(1024)S(1)}, f32[6144]{0:T(1024)}, u32[]{:S(2)}) copy-start(f32[6144]{0:T(1024)} %param.15) | copy-start | bytes 73732
  506.2 454.4 %all-gather.19.cloned.1.call-start = ((), (), s32[]{:S(2)}) async-start(), calls=%async_computation.10 | async-start | bytes 7208960 | tf_op jit(solution)/shard_map/all_gather | solution.py:185
  507.0 569.4 %all-gather.17.cloned.1.call-start = ((), (), s32[]{:S(2)}) async-start(), calls=%async_computation.9 | async-start | bytes 7864320 | tf_op jit(solution)/shard_map/all_gather | solution.py:184
  679.8 87.3 %all-to-all-start.2 = ((bf16[128,4,1920]{0,2,1:T(8,128)(2,1)}), bf16[128,4,1920]{0,2,1:T(8,128)(2,1)S(1)}, u32[]{:S(2)}, u32[]{:S(2)}) async-start(bf16[128,4,1920]{0,2,1:T(8,128)(2,1)} %bitcast.28), calls=%async_computation.3 | async-start | bytes 3932160 | tf_op jit(solution)/shard_map/all_to_all | solution.py:179
  683.4 464.1 %reduce-scatter.5.cloned.1.call-start = ((), (), s32[]{:S(2)}) async-start(), calls=%async_computation.14 | async-start | bytes 8847360 | tf_op jit(solution)/shard_map/reduce_scatter | solution.py:202
  794.8 12.5 copy-start.7
  826.5 55.2 %all-to-all-start.1 = ((f32[128,4,512]{0,2,1:T(8,128)}), f32[128,4,512]{0,2,1:T(8,128)S(1)}, u32[]{:S(2)}, u32[]{:S(2)}) async-start(f32[128,4,512]{0,2,1:T(8,128)} %bitcast.26), calls=%async_computation.1 | async-start | bytes 2097152 | tf_op jit(solution)/shard_map/all_to_all | solution.py:181
  881.7 30.5 %all-to-all-start = ((bf16[128,4,512]{2,0,1:T(8,128)(2,1)}), bf16[128,4,512]{2,0,1:T(8,128)(2,1)S(1)}, u32[]{:S(2)}, u32[]{:S(2)}) async-start(bf16[128,4,512]{2,0,1:T(8,128)(2,1)} %bitcast.79), calls=%async_computation | async-start | bytes 1048576 | tf_op jit(solution)/shard_map/all_to_all | solution.py:178
  885.2 387.9 %reduce-scatter.3.cloned.1.call-start = ((), (), s32[]{:S(2)}) async-start(), calls=%async_computation.12 | async-start | bytes 20201472 | tf_op jit(solution)/shard_map/reduce_scatter | solution.py:199
  1076.4 8.4 copy-start
  1076.4 8.4 copy-start.1
  1273.0 2.8 copy-start.5
  (7 other events, 13.2 us)
Sparse Core Ops, SparseCore 0:
  10.9 147.2 all-gather.12
  161.7 182.9 all-gather.14
  347.6 142.7 all-gather.10
  493.1 152.7 all-gather.8
  647.9 57.1 all-gather.22
  707.1 120.0 all-gather.20
  829.4 131.1 all-gather.18
  962.7 113.6 all-gather.16
  1079.9 67.5 reduce-scatter.4
  1151.5 121.4 reduce-scatter.2
where the time goes:
time: 1300 us; the launch traced here: 1290 us
  waiting for transfers between devices  1050 us (81%)
  matrix products  154 us (12%)
  local copies, waits for them, and re-layouts  32 us (2%)
  other arithmetic  27.1 us (2%)
  between operations  14.7 us (1%)
    all_gather x1, waiting for transfers between devices, on_device(): lax.all_gather(mixer, ('dp', 'fsdp'), axis=0, tiled=True)  174 us
    all_gather x1, waiting for transfers between devices, on_device(): lax.all_gather(w_up, ('dp', 'fsdp'), axis=0, tiled=True)  144 us
    all_gather x1, waiting for transfers between devices, on_device(): lax.all_gather(w_qkv, ('dp', 'fsdp'), axis=0, tiled=True)  137 us
    all_gather x1, waiting for transfers between devices, on_device(): lax.all_gather(w_gate, ('dp', 'fsdp'), axis=0, tiled=True)  125 us
    reduce_scatter x1, waiting for transfers between devices, on_device(): lax.psum_scatter(input_part.astype(jnp.bfloat16), 'fsdp', scatter_dimensi...  122 us
    all_gather x1, waiting for transfers between devices, on_device(): lax.all_gather(grad_proj, 'dp', axis=0, tiled=True)  108 us
    all_to_all x1, waiting for transfers between devices, on_device(): lax.all_to_all(joined, 'dp', split_axis=1, concat_axis=0, tiled=True)  83.2 us
    all_to_all x1, waiting for transfers between devices, on_device(): lax.all_to_all(jnp.transpose(stats), 'dp', split_axis=1, concat_axis=0, t...  50.8 us
  transfers between devices with their start and end apart: 13, of which 11 were waited for; matrix products, arithmetic and copies ran while one was open for 16% of the time, Pallas kernels for 0%

commit v1 on v0

v1 whole, which is shorter than its diff:
```python
import math

import jax
import jax.numpy as jnp
from jax import lax
from jax.sharding import PartitionSpec as P

HD = 64
ROT = 16
EPS = 1e-05
NEG = -1e30
AXES = ("dp", "fsdp")
BF = jnp.bfloat16
F32 = jnp.float32
CONTRACT_ROWS = (((0,), (0,)), ((), ()))
CONTRACT_COLS = (((1,), (1,)), ((), ()))


def block_terms(lengths_row, rows_tok):
    ends = jnp.cumsum(lengths_row)
    place = jnp.arange(rows_tok, dtype=jnp.int32)
    segment = jnp.sum((place[:, None] >= ends[None, :]).astype(jnp.int32), axis=1)
    starts = jnp.concatenate([ends - lengths_row, ends[-1:]])
    labels = jnp.arange(starts.shape[0], dtype=jnp.int32)
    begin = jnp.sum(jnp.where(segment[:, None] == labels[None, :], starts[None, :], 0), axis=1)
    position = (place - begin).astype(F32)
    valid = segment < lengths_row.shape[0]
    label_tok = jnp.where(valid, segment, lengths_row.shape[0] + place)
    allowed = (label_tok[:, None] == label_tok[None, :]) & (place[None, :] <= place[:, None])
    return (position, valid, allowed)


def angles(position):
    half = ROT // 2
    freq = jnp.exp(jnp.arange(half, dtype=F32) * (-2.0 * math.log(10000.0) / ROT))
    turn = position[..., None] * freq
    return (jnp.cos(turn), jnp.sin(turn))


def rotate(heads_in, cosine, sine):
    half = ROT // 2
    first = heads_in[..., :half]
    second = heads_in[..., half:ROT]
    cos_b = cosine[:, :, None, :]
    sin_b = sine[:, :, None, :]
    return jnp.concatenate(
        [first * cos_b - second * sin_b, second * cos_b + first * sin_b, heads_in[..., ROT:]],
        axis=-1,
    )


class Plain:
    def __init__(self, outer, inner):
        self.tp, self.wide, self.cores, self.outer = outer, inner, 1, outer
        self.member = lax.axis_index("dp")
        self.lane = lax.axis_index("fsdp")

    def group_ids(self):
        return jnp.arange(self.tp) * self.wide + self.lane

    def gather_tokens(self, block):
        return lax.all_gather(block, "dp", axis=0, tiled=True)

    def scatter_tokens(self, parts):
        sent = parts.astype(BF).reshape(-1, parts.shape[-1])
        return lax.psum_scatter(sent, "dp", scatter_dimension=0, tiled=True).astype(F32)

    def exchange(self, blocks):
        return lax.all_to_all(blocks, "dp", split_axis=0, concat_axis=0, tiled=True)

    def gather_weights(self, block):
        return lax.all_gather(block, "fsdp", axis=0)

    def scatter_weights(self, blocks):
        flat = blocks.reshape((-1,) + blocks.shape[2:])
        return lax.psum_scatter(flat, "fsdp", scatter_dimension=0, tiled=True)

    def relative(self, blocks, axis):
        return blocks


class Linked:
    def __init__(self, outer, inner):
        self.outer, self.cores, self.wide = outer, 2, inner // 2
        self.tp = outer * 2
        flat = lax.axis_index("fsdp")
        self.core = lax.rem(flat, 2)
        self.lane = flat // 2
        self.depth = lax.axis_index("dp")
        self.member = self.depth * 2 + self.core

    def pairs(self, dz, dk, dc):
        out = []
        for z in range(self.outer):
            for k in range(self.wide):
                for c in range(2):
                    here = (z * self.wide + k) * 2 + c
                    there = ((z ^ dz) * self.wide + (k ^ dk)) * 2 + (c ^ dc)
                    out.append((here, there))
        return out

    def send(self, value, dz=0, dk=0, dc=0):
        return lax.ppermute(value, AXES, self.pairs(dz, dk, dc))

    def group_ids(self):
        ids = []
        for dc in range(2):
            for dz in range(self.outer):
                row = lax.bitwise_xor(self.depth, dz) * self.wide + self.lane
                ids.append(row * 2 + lax.bitwise_xor(self.core, dc))
        return jnp.stack(ids)

    def gather_tokens(self, block):
        parts = [block] + [self.send(block, dz=dz) for dz in range(1, self.outer)]
        mine = jnp.concatenate(parts, axis=0)
        return jnp.concatenate([mine, self.send(mine, dc=1)], axis=0)

    def scatter_tokens(self, parts):
        half = self.outer
        got = self.send(parts[half:].astype(BF), dc=1)
        chip = parts[:half] + got.astype(F32)
        total = chip[0]
        for dz in range(1, self.outer):
            total = total + self.send(chip[dz].astype(BF), dz=dz).astype(F32)
        return total

    def exchange(self, blocks):
        out = blocks
        for step in range(1, self.tp):
            spot = lax.bitwise_xor(self.member, step)
            piece = lax.dynamic_index_in_dim(blocks, spot, 0, keepdims=False)
            got = self.send(piece, dz=step // 2, dc=step % 2)
            out = lax.dynamic_update_index_in_dim(out, got, spot, 0)
        return out

    def gather_weights(self, block):
        half = block.shape[0] // 2
        from_x = self.send(block, dk=1)
        from_y = self.send(block, dk=2)
        low = self.send(from_x[:half], dk=2)
        high = self.send(from_y[half:], dk=1)
        return jnp.stack([block, from_x, from_y, jnp.concatenate([low, high], axis=0)])

    def scatter_weights(self, blocks):
        half = blocks.shape[1] // 2
        low = self.send(blocks[3, :half], dk=1)
        high = self.send(blocks[3, half:], dk=2)
        x_low = self.send(blocks[1, :half], dk=1)
        y_high = self.send(blocks[2, half:], dk=2)
        x_high = self.send((blocks[1, half:].astype(F32) + high.astype(F32)).astype(BF), dk=1)
        y_low = self.send((blocks[2, :half].astype(F32) + low.astype(F32)).astype(BF), dk=2)
        wide = blocks[0].astype(F32)
        low_sum = wide[:half] + x_low.astype(F32) + y_low.astype(F32)
        high_sum = wide[half:] + x_high.astype(F32) + y_high.astype(F32)
        return jnp.concatenate([low_sum, high_sum], axis=0).astype(BF)

    def relative(self, blocks, axis):
        shape = blocks.shape
        split = blocks.reshape(shape[:axis] + (2, 2) + shape[axis + 1 :])
        split = jnp.where(self.lane >= 2, jnp.flip(split, axis), split)
        split = jnp.where(lax.rem(self.lane, 2) == 1, jnp.flip(split, axis + 1), split)
        return split.reshape(shape)


def on_device(
    tokens, ln_gain, ln_shift, w_qkv, b_qkv, w_out, w_gate, w_up, w_down, grad_out, seq_lengths
):
    outer, inner = lax.axis_size("dp"), lax.axis_size("fsdp")
    linked = outer == 4 and inner == 8
    net = Linked(outer, inner) if linked else Plain(outer, inner)
    tp, wide, cores = net.tp, net.wide, net.cores
    rows_tok, width = tokens.shape
    own = w_qkv.shape[0]
    own_ff = w_down.shape[0]
    ff = w_gate.shape[1]
    cols, cols_ff = wide * own, wide * own_ff
    heads = cols // HD
    all_tok = tp * rows_tok

    _, valid, _ = block_terms(seq_lengths[0], rows_tok)
    keep_row = valid.astype(F32)[:, None]
    widened = tokens.astype(F32)
    centered = widened - jnp.mean(widened, axis=1, keepdims=True)
    inv_std = lax.rsqrt(jnp.mean(centered * centered, axis=1, keepdims=True) + EPS)
    scaled = centered * inv_std
    normed = (scaled * ln_gain + ln_shift).astype(BF)
    masked = (grad_out.astype(F32) * keep_row).astype(BF)

    def lanes_first(x):
        split = x.reshape(rows_tok, outer, wide, cores * own)
        return net.relative(jnp.swapaxes(split, 1, 2), 1).reshape(rows_tok, width)

    def lanes_back(x):
        split = net.relative(x.reshape(rows_tok, wide, outer, cores * own), 1)
        return jnp.swapaxes(split, 1, 2).reshape(rows_tok, width)

    def pack(w, groups, piece):
        split = w.reshape(own, groups, outer, wide, cores, piece)
        return jnp.transpose(split, (2, 4, 0, 1, 3, 5)).reshape(tp, own, groups * wide * piece)

    packed = jnp.concatenate(
        [pack(w_qkv, 3, own), pack(w_gate, 1, own_ff), pack(w_up, 1, own_ff)], axis=2
    )
    entry = net.exchange(packed).reshape(tp * own, -1)
    mixer = net.gather_weights(jnp.concatenate([w_out, w_down], axis=0))
    mixer = net.relative(mixer, 0)
    mixer = jnp.concatenate(
        [mixer[:, :own].reshape(cols, width), mixer[:, own:].reshape(cols_ff, width)], axis=0
    )
    entry = net.gather_weights(entry).reshape(width, -1)

    normed_all = net.gather_tokens(lanes_first(normed))
    masked_all = net.gather_tokens(masked)
    lengths = jnp.take(lax.all_gather(seq_lengths, AXES, axis=0, tiled=True), net.group_ids(), 0)
    position, _, allowed = jax.vmap(lambda row: block_terms(row, rows_tok))(lengths)
    cosine, sine = angles(position)

    bias = lax.dynamic_index_in_dim(
        jnp.transpose(b_qkv.reshape(3, outer, wide, cores, own), (1, 3, 0, 2, 4)).reshape(tp, -1),
        net.member,
        0,
        keepdims=False,
    )
    proj = jnp.dot(normed_all, entry, preferred_element_type=F32)
    proj_gate = proj[:, 3 * cols : 3 * cols + cols_ff]
    proj_up = proj[:, 3 * cols + cols_ff :]
    split_qkv = (proj[:, : 3 * cols] + bias).reshape(tp, rows_tok, 3, heads, HD)
    query = rotate(split_qkv[:, :, 0], cosine, sine).astype(BF)
    keys = rotate(split_qkv[:, :, 1], cosine, sine).astype(BF)
    values = split_qkv[:, :, 2].astype(BF)
    scores = jnp.einsum("bqhd,bkhd->bhqk", query, keys, preferred_element_type=F32) * 0.125
    scores = jnp.where(allowed[:, None], scores, NEG)
    peak = jnp.max(scores, axis=3, keepdims=True)
    lifted = jnp.exp(scores - peak)
    probs = lifted / jnp.sum(lifted, axis=3, keepdims=True)
    probs_low = probs.astype(BF)
    attended = jnp.einsum("bhqk,bkhd->bqhd", probs_low, values, preferred_element_type=F32)
    attended = attended.reshape(all_tok, cols).astype(BF)
    sigma = jax.nn.sigmoid(proj_gate)
    activ = proj_gate * sigma
    hidden = (activ * proj_up).astype(BF)
    joined = jnp.concatenate([attended, hidden], axis=1)

    branch = jnp.dot(joined, mixer, preferred_element_type=F32)
    branch = net.scatter_tokens(branch.reshape(tp, rows_tok, width))
    output = (widened + keep_row * branch).astype(BF)

    back = lax.dot_general(masked_all, mixer, CONTRACT_COLS, preferred_element_type=F32)
    grad_mixed = back[:, :cols].astype(BF).reshape(tp, rows_tok, heads, HD)
    grad_hid = back[:, cols:]
    grad_probs = jnp.einsum("bqhd,bkhd->bhqk", grad_mixed, values, preferred_element_type=F32)
    inner_sum = jnp.sum(probs * grad_probs, axis=3, keepdims=True)
    grad_scores = (probs * (grad_probs - inner_sum)).astype(BF)
    grad_query = (
        jnp.einsum("bhqk,bkhd->bqhd", grad_scores, keys, preferred_element_type=F32) * 0.125
    )
    grad_keys = (
        jnp.einsum("bhqk,bqhd->bkhd", grad_scores, query, preferred_element_type=F32) * 0.125
    )
    grad_values = jnp.einsum("bhqk,bqhd->bkhd", probs_low, grad_mixed, preferred_element_type=F32)
    grad_proj = jnp.stack(
        [rotate(grad_query, cosine, -sine), rotate(grad_keys, cosine, -sine), grad_values], axis=2
    )
    grad_proj = grad_proj.reshape(all_tok, 3 * cols).astype(BF)
    slope = sigma * (1.0 + proj_gate * (1.0 - sigma))
    grad_gate = (grad_hid * proj_up * slope).astype(BF)
    grad_up = (grad_hid * activ).astype(BF)
    grad_entry = jnp.concatenate([grad_proj, grad_gate, grad_up], axis=1)

    mixer_part = lax.dot_general(
        joined, masked_all, CONTRACT_ROWS, preferred_element_type=F32
    ).astype(BF)
    mixer_part = jnp.concatenate(
        [
            mixer_part[:cols].reshape(wide, own, width),
            mixer_part[cols:].reshape(wide, own_ff, width),
        ],
        axis=1,
    )
    mixer_sum = net.scatter_weights(net.relative(mixer_part, 0)).astype(F32)
    entry_part = lax.dot_general(
        normed_all, grad_entry, CONTRACT_ROWS, preferred_element_type=F32
    ).astype(BF)
    entry_sum = net.scatter_weights(entry_part.reshape(wide, tp * own, -1))
    entry_sum = net.exchange(entry_sum.reshape(tp, own, -1)).astype(F32)

    def unpack(part, groups, piece):
        split = part.reshape(outer, cores, own, groups, wide, piece)
        return jnp.transpose(split, (2, 3, 0, 4, 1, 5)).reshape(own, -1)

    grad_w_qkv = unpack(entry_sum[:, :, : 3 * cols], 3, own)
    grad_w_gate = unpack(entry_sum[:, :, 3 * cols : 3 * cols + cols_ff], 1, own_ff)
    grad_w_up = unpack(entry_sum[:, :, 3 * cols + cols_ff :], 1, own_ff)

    grad_norm = lax.dot_general(grad_entry, entry, CONTRACT_COLS, preferred_element_type=F32)
    grad_norm = lanes_back(net.scatter_tokens(grad_norm.reshape(tp, rows_tok, width)))
    lifted_grad = grad_norm * ln_gain
    grad_in = inv_std * (
        lifted_grad
        - jnp.mean(lifted_grad, axis=1, keepdims=True)
        - scaled * jnp.mean(lifted_grad * scaled, axis=1, keepdims=True)
    )
    grad_tokens = (grad_out.astype(F32) + grad_in).astype(BF)

    shards = outer * inner
    gain_part = jnp.sum(grad_norm * scaled, axis=0)
    shift_part = jnp.sum(grad_norm, axis=0)
    bias_part = jnp.sum(grad_proj.astype(F32), axis=0)
    bias_full = lax.dynamic_update_index_in_dim(
        jnp.zeros((tp, 3 * cols), F32), bias_part, net.member, 0
    )
    bias_full = jnp.transpose(bias_full.reshape(outer, cores, 3, wide, own), (2, 0, 3, 1, 4))
    stats = jnp.concatenate(
        [
            gain_part.reshape(shards, own),
            shift_part.reshape(shards, own),
            bias_full.reshape(shards, 3 * own),
        ],
        axis=1,
    )
    stats = lax.psum_scatter(stats.reshape(-1), AXES, scatter_dimension=0, tiled=True)
    return (
        output,
        grad_tokens,
        grad_w_qkv,
        mixer_sum[:own],
        grad_w_gate,
        grad_w_up,
        mixer_sum[own:],
        stats[:own],
        stats[own : 2 * own],
        stats[2 * own :],
    )


def solution(mesh):
    rows = P(AXES, None)
    return jax.shard_map(
        on_device,
        mesh=mesh,
        in_specs=(rows, P(), P(), rows, P(), rows, rows, rows, rows, rows, rows),
        out_specs=(rows,) * 7 + (P(AXES),) * 3,
        check_vma=False,
    )
```

time: 1300 us -> 700 us (0.54)
  waiting for transfers between devices: 1050 us -> 283 us
  local copies, waits for them, and re-layouts: 32 us -> 138 us
  blocking collectives: 0 us -> 86.7 us
  matrix products: 154 us -> 67.7 us
  other arithmetic: 27.1 us -> 63.9 us
  starting transfers between devices: 11.6 us -> 48.4 us
    all_gather x8 -> x0, waiting for transfers between devices: 730 us -> none  [the longest x1 174 us: on_device(): lax.all_gather(mixer, ('dp', 'fsdp'), axis=0, tiled=True)]
    ppermute x0 -> x50, waiting for transfers between devices: none -> 283 us  [send(): return lax.ppermute(value, AXES, self.pairs(dz, dk, dc))]
    all_to_all x3 -> x0, waiting for transfers between devices: 161 us -> none  [the longest x1 83.2 us: on_device(): lax.all_to_all(joined, 'dp', split_axis=1, concat_axis=0, tiled=True)]
    reduce_scatter x2 -> x0, waiting for transfers between devices: 155 us -> none  [the longest x1 122 us: on_device(): lax.psum_scatter(input_part.astype(jnp.bfloat16), 'fsdp', scatter_dimensi...]
    dot_general x18 -> x11, matrix products: 154 us -> 65.8 us  [the longest x1 18.3 us: on_device(): lax.dot_general(normed_all, grad_entry, CONTRACT_ROWS, preferred_element_...]
    reshape x3 -> x29, local copies, waits for them, and re-layouts: 6.15 us -> 57.6 us  [the longest x6 19 us: unpack(): split = part.reshape(outer, cores, own, groups, wide, piece)]
    ppermute x0 -> x50, starting transfers between devices: none -> 48.4 us  [send(): return lax.ppermute(value, AXES, self.pairs(dz, dk, dc))]
    all_gather x0 -> x1, blocking collectives: none -> 46.4 us  [on_device(): lax.all_gather(seq_lengths, AXES, axis=0, tiled=True)]
  transfers between devices with their start and end apart: 13 -> 50, of which waited for: 11 -> 21; matrix products, arithmetic and copies ran while one was open for 16% -> 17% of each run, Pallas kernels for 0% -> 0%
where the time goes in v1:
time: 700 us; the launch traced here: 690 us
  waiting for transfers between devices  283 us (40%)
  local copies, waits for them, and re-layouts  138 us (20%)
  blocking collectives  86.7 us (12%)
  matrix products  67.7 us (10%)
  other arithmetic  63.9 us (9%)
  starting transfers between devices  48.4 us (7%)
    ppermute x50, waiting for transfers between devices, send(): return lax.ppermute(value, AXES, self.pairs(dz, dk, dc))  283 us
    ppermute x50, starting transfers between devices, send(): return lax.ppermute(value, AXES, self.pairs(dz, dk, dc))  48.4 us
    all_gather x1, blocking collectives, on_device(): lax.all_gather(seq_lengths, AXES, axis=0, tiled=True)  46.4 us
    unnamed x1, blocking collectives  40.3 us
    unnamed x134, local copies, waits for them, and re-layouts  24.2 us
    reshape x6, local copies, waits for them, and re-layouts, unpack(): split = part.reshape(outer, cores, own, groups, wide, piece)  19 us
    dot_general x1, matrix products, on_device(): lax.dot_general(normed_all, grad_entry, CONTRACT_ROWS, preferred_element_...  18.3 us
  transfers between devices with their start and end apart: 50, of which 21 were waited for; matrix products, arithmetic and copies ran while one was open for 17% of the time, Pallas kernels for 0%

profile of v1, /device:TPU:0, one launch (start us, length us, event | category | flops | bytes accessed | tf_op | source)
XLA Modules:
  0.0 690.5 jit_solution(16281176562250863124)
XLA Ops:
  7.7 5.0 collective-permute-start.2
  34.7 46.4 %all-gather = s32[32,1,4]{2,1,0:T(1,128)S(1)} all-gather(s32[1,1,4]{2,1,0:T(1,128)S(1)} %bitcast.319), channel_id=1, replica_groups=mesh['dp'=4,'fsdp'=8] {'dp','fsdp'}, dimensions={0}, use_global_device_ids=true | all-gather | bytes 528 | tf_op jit(solution)/shard_map/all_gather | solution.py:214
  109.9 36.8 %collective-permute-done.24 = bf16[128,2048]{1,0:T(8,128)(2,1)S(1)} collective-permute-done((bf16[128,2048]{1,0:T(8,128)(2,1)S(1)}, bf16[128,2048]{1,0:T(8,128)(2,1)S(1)}, u32[]{:S(2)}, u32[]{:S(2)}) %collective-permute-start.24) | collective-permute-done | bytes 524320 | tf_op jit(solution)/shard_map/ppermute | solution.py:103
  150.0 6.1 collective-permute-done.5
  156.1 10.7 %collective-permute-done.6 = bf16[64,2176]{1,0:T(8,128)(2,1)S(1)} collective-permute-done((bf16[64,2176]{1,0:T(8,128)(2,1)S(1)}, bf16[64,2176]{1,0:T(8,128)(2,1)S(1)}, u32[]{:S(2)}, u32[]{:S(2)}) %collective-permute-start.6) | collective-permute-done | bytes 278560 | tf_op jit(solution)/shard_map/ppermute | solution.py:103
  166.8 14.6 %collective-permute-done.7 = bf16[64,2176]{1,0:T(8,128)(2,1)S(1)} collective-permute-done((bf16[64,2176]{1,0:T(8,128)(2,1)S(1)}, bf16[64,2176]{1,0:T(8,128)(2,1)S(1)}, u32[]{:S(2)}, u32[]{:S(2)}) %collective-permute-start.7) | collective-permute-done | bytes 278560 | tf_op jit(solution)/shard_map/ppermute | solution.py:103
  181.4 12.7 %collective-permute-done.8 = bf16[64,2176]{1,0:T(8,128)(2,1)S(1)} collective-permute-done((bf16[64,2176]{1,0:T(8,128)(2,1)S(1)}, bf16[64,2176]{1,0:T(8,128)(2,1)S(1)}, u32[]{:S(2)}, u32[]{:S(2)}) %collective-permute-start.8) | collective-permute-done | bytes 278560 | tf_op jit(solution)/shard_map/ppermute | solution.py:103
  199.8 9.7 %collective-permute-done.18 = bf16[120,2048]{1,0:T(8,128)(2,1)S(1)} collective-permute-done((bf16[120,2048]{1,0:T(8,128)(2,1)S(1)}, bf16[120,2048]{1,0:T(8,128)(2,1)S(1)}, u32[]{:S(2)}, u32[]{:S(2)}) %collective-permute-start.18) | collective-permute-done | bytes 491552 | tf_op jit(solution)/shard_map/ppermute | solution.py:103
  215.1 41.8 %collective-permute-done.12 = bf16[512,2176]{1,0:T(8,128)(2,1)S(1)} collective-permute-done((bf16[512,2176]{1,0:T(8,128)(2,1)S(1)}, bf16[512,2176]{1,0:T(8,128)(2,1)S(1)}, u32[]{:S(2)}, u32[]{:S(2)}) %collective-permute-start.12) | collective-permute-done | bytes 2228256 | tf_op jit(solution)/shard_map/ppermute | solution.py:103
  275.0 8.9 %collective-permute-done.14 = bf16[256,2176]{1,0:T(8,128)(2,1)S(1)} collective-permute-done((bf16[256,2176]{1,0:T(8,128)(2,1)}, bf16[256,2176]{1,0:T(8,128)(2,1)S(1)}, u32[]{:S(2)}, u32[]{:S(2)}) %collective-permute-start.14) | collective-permute-done | bytes 1114144 | tf_op jit(solution)/shard_map/ppermute | solution.py:103
  290.3 9.9 %fusion.84 = f32[1024,2176]{1,0:T(8,128)S(1)} fusion(bf16[1024,2048]{1,0:T(8,128)(2,1)S(1)} %copy-done.48, bf16[2048,2176]{1,0:T(8,128)(2,1)S(1)} %bitcast.290), kind=kOutput, calls=%fused_computation.251 | convolution fusion | flops 9126805504 | bytes 22020096 | tf_op jit(solution)/shard_map/dot_general | solution.py:224
  314.4 5.4 multiply_convert_fusion.1
  334.0 7.1 %convolution_convert_fusion.1 = bf16[960,2048]{1,0:T(8,128)(2,1)S(1)} fusion(bf16[1024,2048]{1,0:T(8,128)(2,1)} %copy-done.46, bf16[1024,704]{1,0:T(8,128)(2,1)} %get-tuple-element.30, bf16[1024,256]{1,0:T(8,128)(2,1)} %reshape.681), kind=kOutput, calls=%fused_computation.16 | convolution fusion | flops 4032430080 | bytes 10092544 | tf_op jit(solution)/shard_map/dot_general | solution.py:270
  358.4 13.6 %fusion.11 = f32[1024,2048]{1,0:T(8,128)S(1)} fusion(bf16[2048,2176]{1,0:T(8,128)(2,1)} %bitcast.291, bf16[1024,704]{0,1:T(8,128)(2,1)} %copy.150, bf16[1024,704]{0,1:T(8,128)(2,1)S(1)} %copy-done.23, bf16[1024,768]{0,1:T(8,128)(2,1)} %bitcast.309), kind=kOutput, calls=%fused_computation.51 | convolution fusion | flops 9140174848 | bytes 21757952 | tf_op jit(solution)/shard_map/dot_general | solution.py:295
  372.1 18.3 %convolution_convert_fusion = bf16[2048,2176]{1,0:T(8,128)(2,1)} fusion(bf16[1024,2048]{1,0:T(8,128)(2,1)} %constant_dynamic-update-slice_fusion, bf16[1024,704]{0,1:T(8,128)(2,1)} %copy.150, bf16[1024,704]{0,1:T(8,128)(2,1)S(1)} %copy-done.23, bf16[1024,768]{0,1:T(8,128)(2,1)} %bitcast.310), kind=kOutput, calls=%fused_computation.2 | convolution fusion | flops 9144631296 | bytes 17563648 | tf_op jit(solution)/shard_map/dot_general | solution.py:281
  406.0 6.0 fusion.3
  427.7 23.3 %collective-permute-done.46 = bf16[120,2048]{1,0:T(8,128)(2,1)} collective-permute-done((bf16[120,2048]{1,0:T(8,128)(2,1)}, bf16[120,2048]{1,0:T(8,128)(2,1)}, u32[]{:S(2)}, u32[]{:S(2)}) %collective-permute-start.46) | collective-permute-done | bytes 491552 | tf_op jit(solution)/shard_map/ppermute | solution.py:103
  468.8 10.6 %collective-permute-done.31 = bf16[256,2176]{1,0:T(8,128)(2,1)S(1)} collective-permute-done((bf16[256,2176]{1,0:T(8,128)(2,1)}, bf16[256,2176]{1,0:T(8,128)(2,1)S(1)}, u32[]{:S(2)}, u32[]{:S(2)}) %collective-permute-start.31) | collective-permute-done | bytes 1114144 | tf_op jit(solution)/shard_map/ppermute | solution.py:103
  484.9 22.4 %collective-permute-done.33 = bf16[256,2176]{1,0:T(8,128)(2,1)S(1)} collective-permute-done((bf16[256,2176]{1,0:T(8,128)(2,1)S(1)}, bf16[256,2176]{1,0:T(8,128)(2,1)S(1)}, u32[]{:S(2)}, u32[]{:S(2)}) %collective-permute-start.33) | collective-permute-done | bytes 1114144 | tf_op jit(solution)/shard_map/ppermute | solution.py:103
  515.5 42.7 %collective-permute-done.29 = bf16[128,2048]{1,0:T(8,128)(2,1)S(1)} collective-permute-done((bf16[128,2048]{1,0:T(8,128)(2,1)S(1)}, bf16[128,2048]{1,0:T(8,128)(2,1)S(1)}, u32[]{:S(2)}, u32[]{:S(2)}) %collective-permute-start.29) | collective-permute-done | bytes 524320 | tf_op jit(solution)/shard_map/ppermute | solution.py:103
  577.3 18.4 %collective-permute-done.21 = bf16[128,2048]{1,0:T(8,128)(2,1)} collective-permute-done((bf16[128,2048]{1,0:T(8,128)(2,1)}, bf16[128,2048]{1,0:T(8,128)(2,1)}, u32[]{:S(2)}, u32[]{:S(2)}) %collective-permute-start.21) | collective-permute-done | bytes 524320 | tf_op jit(solution)/shard_map/ppermute | solution.py:103
  599.6 40.3 %all-reduce = f32[10240]{0:T(1024)S(1)} all-reduce(f32[10240]{0:T(1024)S(1)} %reshape.666), channel_id=2, replica_groups=mesh['dp'=4,'fsdp'=8] {'dp','fsdp'}, use_global_device_ids=true, to_apply=%region_15.16.clone | all-reduce | flops 10240 | bytes 81920
  642.1 7.4 %collective-permute-done.39 = bf16[64,2176]{1,0:T(8,128)(2,1)S(1)} collective-permute-done((bf16[64,2176]{1,0:T(8,128)(2,1)}, bf16[64,2176]{1,0:T(8,128)(2,1)S(1)}, u32[]{:S(2)}, u32[]{:S(2)}) %collective-permute-start.39) | collective-permute-done | bytes 278560 | tf_op jit(solution)/shard_map/ppermute | solution.py:103
  674.3 5.2 reshape.656
  (391 shorter events, 264.8 us)
Async XLA Ops:
  7.7 89.2 %collective-permute-start.2 = (bf16[128,2048]{1,0:T(8,128)(2,1)}, bf16[128,2048]{1,0:T(8,128)(2,1)}, u32[]{:S(2)}, u32[]{:S(2)}) collective-permute-start(bf16[128,2048]{1,0:T(8,128)(2,1)} %reshape_reshape.6), channel_id=1, source_target_pairs={{0,24},{1,25},{2,26},{3,27},{4,28},{5,29},{6,30},{7,31},{8,16},{9,... | collective-permute-start | bytes 1572872 | tf_op jit(solution)/shard_map/ppermute | solution.py:103
  12.7 78.8 %collective-permute-start.1 = (bf16[128,2048]{1,0:T(8,128)(2,1)}, bf16[128,2048]{1,0:T(8,128)(2,1)}, u32[]{:S(2)}, u32[]{:S(2)}) collective-permute-start(bf16[128,2048]{1,0:T(8,128)(2,1)} %reshape_reshape.6), channel_id=1, source_target_pairs={{0,16},{1,17},{2,18},{3,19},{4,20},{5,21},{6,22},{7,23},{8,24},{9,... | collective-permute-start | bytes 1572872 | tf_op jit(solution)/shard_map/ppermute | solution.py:103
  12.7 75.4 %collective-permute-start = (bf16[128,2048]{1,0:T(8,128)(2,1)}, bf16[128,2048]{1,0:T(8,128)(2,1)}, u32[]{:S(2)}, u32[]{:S(2)}) collective-permute-start(bf16[128,2048]{1,0:T(8,128)(2,1)} %reshape_reshape.6), channel_id=1, source_target_pairs={{0,8},{1,9},{2,10},{3,11},{4,12},{5,13},{6,14},{7,15},{8,0},{9,1},... | collective-permute-start | bytes 1572872 | tf_op jit(solution)/shard_map/ppermute | solution.py:103
  14.9 179.4 %collective-permute-start.16 = (bf16[240,2048]{1,0:T(8,128)(2,1)}, bf16[240,2048]{1,0:T(8,128)(2,1)}, u32[]{:S(2)}, u32[]{:S(2)}) collective-permute-start(bf16[240,2048]{1,0:T(8,128)(2,1)} %constant_dynamic-update-slice_fusion.5), channel_id=1, source_target_pairs={{0,4},{1,5},{2,6},{3,7},{4,0},{5,1},{6,2},{7,3},{8,12},{9,13},{10,... | collective-permute-start | bytes 2949128 | tf_op jit(solution)/shard_map/ppermute | solution.py:103
  34.4 52.3 %collective-permute-start.4 = (bf16[64,2176]{1,0:T(8,128)(2,1)}, bf16[64,2176]{1,0:T(8,128)(2,1)}, u32[]{:S(2)}, u32[]{:S(2)}) collective-permute-start(bf16[64,2176]{1,0:T(8,128)(2,1)} %dynamic-slice_bitcast_fusion.13), channel_id=1, source_target_pairs={{0,1},{1,0},{2,3},{3,2},{4,5},{5,4},{6,7},{7,6},{8,9},{9,8},{10,11... | collective-permute-start | bytes 835592 | tf_op jit(solution)/shard_map/ppermute | solution.py:103
  86.7 109.2 %collective-permute-start.15 = (bf16[240,2048]{1,0:T(8,128)(2,1)}, bf16[240,2048]{1,0:T(8,128)(2,1)S(1)}, u32[]{:S(2)}, u32[]{:S(2)}) collective-permute-start(bf16[240,2048]{1,0:T(8,128)(2,1)} %constant_dynamic-update-slice_fusion.5), channel_id=1, source_target_pairs={{0,2},{1,3},{2,0},{3,1},{4,6},{5,7},{6,4},{7,5},{8,10},{9,11},{10,... | collective-permute-start | bytes 2949128 | tf_op jit(solution)/shard_map/ppermute | solution.py:103
  91.5 55.4 %collective-permute-start.25 = (bf16[128,2048]{1,0:T(8,128)(2,1)S(1)}, bf16[128,2048]{1,0:T(8,128)(2,1)S(1)}, u32[]{:S(2)}, u32[]{:S(2)}) collective-permute-start(bf16[128,2048]{1,0:T(8,128)(2,1)S(1)} %get-tuple-element.19), channel_id=1, source_target_pairs={{0,24},{1,25},{2,26},{3,27},{4,28},{5,29},{6,30},{7,31},{8,16},{9,... | collective-permute-start | bytes 1572872 | tf_op jit(solution)/shard_map/ppermute | solution.py:103
  96.9 49.9 %collective-permute-start.24 = (bf16[128,2048]{1,0:T(8,128)(2,1)S(1)}, bf16[128,2048]{1,0:T(8,128)(2,1)S(1)}, u32[]{:S(2)}, u32[]{:S(2)}) collective-permute-start(bf16[128,2048]{1,0:T(8,128)(2,1)S(1)} %get-tuple-element.19), channel_id=1, source_target_pairs={{0,16},{1,17},{2,18},{3,19},{4,20},{5,21},{6,22},{7,23},{8,24},{9,... | collective-permute-start | bytes 1572872 | tf_op jit(solution)/shard_map/ppermute | solution.py:103
  102.8 93.6 %collective-permute-start.10 = (bf16[64,2176]{1,0:T(8,128)(2,1)S(1)}, bf16[64,2176]{1,0:T(8,128)(2,1)S(1)}, u32[]{:S(2)}, u32[]{:S(2)}) collective-permute-start(bf16[64,2176]{1,0:T(8,128)(2,1)S(1)} %get-tuple-element.50), channel_id=1, source_target_pairs={{0,25},{1,24},{2,27},{3,26},{4,29},{5,28},{6,31},{7,30},{8,17},{9,... | collective-permute-start | bytes 835592 | tf_op jit(solution)/shard_map/ppermute | solution.py:103
  146.9 47.3 %collective-permute-start.9 = (bf16[64,2176]{1,0:T(8,128)(2,1)S(1)}, bf16[64,2176]{1,0:T(8,128)(2,1)S(1)}, u32[]{:S(2)}, u32[]{:S(2)}) collective-permute-start(bf16[64,2176]{1,0:T(8,128)(2,1)S(1)} %get-tuple-element.51), channel_id=1, source_target_pairs={{0,24},{1,25},{2,26},{3,27},{4,28},{5,29},{6,30},{7,31},{8,16},{9,... | collective-permute-start | bytes 835592 | tf_op jit(solution)/shard_map/ppermute | solution.py:103
  196.4 60.5 %collective-permute-start.12 = (bf16[512,2176]{1,0:T(8,128)(2,1)S(1)}, bf16[512,2176]{1,0:T(8,128)(2,1)S(1)}, u32[]{:S(2)}, u32[]{:S(2)}) collective-permute-start(bf16[512,2176]{1,0:T(8,128)(2,1)S(1)} %bitcast.268), channel_id=1, source_target_pairs={{0,4},{1,5},{2,6},{3,7},{4,0},{5,1},{6,2},{7,3},{8,12},{9,13},{10,... | collective-permute-start | bytes 6684680 | tf_op jit(solution)/shard_map/ppermute | solution.py:103
  198.1 61.7 %collective-permute-start.11 = (bf16[512,2176]{1,0:T(8,128)(2,1)S(1)}, bf16[512,2176]{1,0:T(8,128)(2,1)S(1)}, u32[]{:S(2)}, u32[]{:S(2)}) collective-permute-start(bf16[512,2176]{1,0:T(8,128)(2,1)S(1)} %bitcast.269), channel_id=1, source_target_pairs={{0,2},{1,3},{2,0},{3,1},{4,6},{5,7},{6,4},{7,5},{8,10},{9,11},{10,... | collective-permute-start | bytes 6684680 | tf_op jit(solution)/shard_map/ppermute | solution.py:103
  209.5 62.4 %collective-permute-start.3 = (bf16[512,2048]{1,0:T(8,128)(2,1)}, bf16[512,2048]{1,0:T(8,128)(2,1)}, u32[]{:S(2)}, u32[]{:S(2)}) collective-permute-start(bf16[512,2048]{1,0:T(8,128)(2,1)} %pad_maximum_fusion.8), channel_id=1, source_target_pairs={{0,1},{1,0},{2,3},{3,2},{4,5},{5,4},{6,7},{7,6},{8,9},{9,8},{10,11... | collective-permute-start | bytes 6291464 | tf_op jit(solution)/shard_map/ppermute | solution.py:103
  400.2 62.1 %collective-permute-start.27 = (bf16[4,128,2048]{2,1,0:T(8,128)(2,1)}, bf16[4,128,2048]{2,1,0:T(8,128)(2,1)}, u32[]{:S(2)}, u32[]{:S(2)}) collective-permute-start(bf16[4,128,2048]{2,1,0:T(8,128)(2,1)} %bitcast.73), channel_id=1, source_target_pairs={{0,1},{1,0},{2,3},{3,2},{4,5},{5,4},{6,7},{7,6},{8,9},{9,8},{10,11... | collective-permute-start | bytes 6291464 | tf_op jit(solution)/shard_map/ppermute | solution.py:103
  461.4 45.9 %collective-permute-start.33 = (bf16[256,2176]{1,0:T(8,128)(2,1)S(1)}, bf16[256,2176]{1,0:T(8,128)(2,1)S(1)}, u32[]{:S(2)}, u32[]{:S(2)}) collective-permute-start(bf16[256,2176]{1,0:T(8,128)(2,1)S(1)} %get-tuple-element.28), channel_id=1, source_target_pairs={{0,4},{1,5},{2,6},{3,7},{4,0},{5,1},{6,2},{7,3},{8,12},{9,13},{10,... | collective-permute-start | bytes 3342344 | tf_op jit(solution)/shard_map/ppermute | solution.py:103
  465.7 47.4 %collective-permute-start.28 = (bf16[128,2048]{1,0:T(8,128)(2,1)S(1)}, bf16[128,2048]{1,0:T(8,128)(2,1)S(1)}, u32[]{:S(2)}, u32[]{:S(2)}) collective-permute-start(bf16[128,2048]{1,0:T(8,128)(2,1)S(1)} %get-tuple-element.57), channel_id=1, source_target_pairs={{0,8},{1,9},{2,10},{3,11},{4,12},{5,13},{6,14},{7,15},{8,0},{9,1},... | collective-permute-start | bytes 1572872 | tf_op jit(solution)/shard_map/ppermute | solution.py:103
  484.9 73.3 %collective-permute-start.29 = (bf16[128,2048]{1,0:T(8,128)(2,1)S(1)}, bf16[128,2048]{1,0:T(8,128)(2,1)S(1)}, u32[]{:S(2)}, u32[]{:S(2)}) collective-permute-start(bf16[128,2048]{1,0:T(8,128)(2,1)S(1)} %get-tuple-element.59), channel_id=1, source_target_pairs={{0,16},{1,17},{2,18},{3,19},{4,20},{5,21},{6,22},{7,23},{8,24},{9,... | collective-permute-start | bytes 1572872 | tf_op jit(solution)/shard_map/ppermute | solution.py:103
  509.5 67.7 %collective-permute-start.20 = (bf16[128,2048]{1,0:T(8,128)(2,1)}, bf16[128,2048]{1,0:T(8,128)(2,1)}, u32[]{:S(2)}, u32[]{:S(2)}) collective-permute-start(bf16[128,2048]{1,0:T(8,128)(2,1)} %get-tuple-element.60), channel_id=1, source_target_pairs={{0,8},{1,9},{2,10},{3,11},{4,12},{5,13},{6,14},{7,15},{8,0},{9,1},... | collective-permute-start | bytes 1572872 | tf_op jit(solution)/shard_map/ppermute | solution.py:103
  509.9 67.3 %collective-permute-start.22 = (bf16[128,2048]{1,0:T(8,128)(2,1)}, bf16[128,2048]{1,0:T(8,128)(2,1)}, u32[]{:S(2)}, u32[]{:S(2)}) collective-permute-start(bf16[128,2048]{1,0:T(8,128)(2,1)} %get-tuple-element.61), channel_id=1, source_target_pairs={{0,24},{1,25},{2,26},{3,27},{4,28},{5,29},{6,30},{7,31},{8,16},{9,... | collective-permute-start | bytes 1572872 | tf_op jit(solution)/shard_map/ppermute | solution.py:103
  513.1 82.6 %collective-permute-start.21 = (bf16[128,2048]{1,0:T(8,128)(2,1)}, bf16[128,2048]{1,0:T(8,128)(2,1)}, u32[]{:S(2)}, u32[]{:S(2)}) collective-permute-start(bf16[128,2048]{1,0:T(8,128)(2,1)} %get-tuple-element.62), channel_id=1, source_target_pairs={{0,16},{1,17},{2,18},{3,19},{4,20},{5,21},{6,22},{7,23},{8,24},{9,... | collective-permute-start | bytes 1572872 | tf_op jit(solution)/shard_map/ppermute | solution.py:103
  514.1 138.4 %collective-permute-start.43 = (bf16[64,2176]{1,0:T(8,128)(2,1)S(1)}, bf16[64,2176]{1,0:T(8,128)(2,1)}, u32[]{:S(2)}, u32[]{:S(2)}) collective-permute-start(bf16[64,2176]{1,0:T(8,128)(2,1)S(1)} %get-tuple-element.43), channel_id=1, source_target_pairs={{0,25},{1,24},{2,27},{3,26},{4,29},{5,28},{6,31},{7,30},{8,17},{9,... | collective-permute-start | bytes 835592 | tf_op jit(solution)/shard_map/ppermute | solution.py:103
  558.2 93.3 %collective-permute-start.42 = (bf16[64,2176]{1,0:T(8,128)(2,1)}, bf16[64,2176]{1,0:T(8,128)(2,1)}, u32[]{:S(2)}, u32[]{:S(2)}) collective-permute-start(bf16[64,2176]{1,0:T(8,128)(2,1)} %get-tuple-element.44), channel_id=1, source_target_pairs={{0,24},{1,25},{2,26},{3,27},{4,28},{5,29},{6,30},{7,31},{8,16},{9,... | collective-permute-start | bytes 835592 | tf_op jit(solution)/shard_map/ppermute | solution.py:103
  577.2 73.4 %collective-permute-start.41 = (bf16[64,2176]{1,0:T(8,128)(2,1)}, bf16[64,2176]{1,0:T(8,128)(2,1)}, u32[]{:S(2)}, u32[]{:S(2)}) collective-permute-start(bf16[64,2176]{1,0:T(8,128)(2,1)} %get-tuple-element.45), channel_id=1, source_target_pairs={{0,17},{1,16},{2,19},{3,18},{4,21},{5,20},{6,23},{7,22},{8,25},{9,... | collective-permute-start | bytes 835592 | tf_op jit(solution)/shard_map/ppermute | solution.py:103
  577.2 72.4 %collective-permute-start.40 = (bf16[64,2176]{1,0:T(8,128)(2,1)}, bf16[64,2176]{1,0:T(8,128)(2,1)}, u32[]{:S(2)}, u32[]{:S(2)}) collective-permute-start(bf16[64,2176]{1,0:T(8,128)(2,1)} %get-tuple-element.46), channel_id=1, source_target_pairs={{0,16},{1,17},{2,18},{3,19},{4,20},{5,21},{6,22},{7,23},{8,24},{9,... | collective-permute-start | bytes 835592 | tf_op jit(solution)/shard_map/ppermute | solution.py:103
  (89 other events, 1314.2 us)

commit v2 on v1

v2 whole, which is shorter than its diff:
```python
import functools
import math

import jax
import jax.numpy as jnp
from jax import lax
from jax.experimental import pallas as pl
from jax.experimental.pallas import tpu as pltpu
from jax.sharding import PartitionSpec as P

HD = 64
ROT = 16
EPS = 1e-05
NEG = -1e30
TILE = 128
AXES = ("dp", "fsdp")
BF = jnp.bfloat16
F32 = jnp.float32
CONTRACT_ROWS = (((0,), (0,)), ((), ()))
CONTRACT_COLS = (((1,), (1,)), ((), ()))


def block_terms(lengths_row, rows_tok):
    ends = jnp.cumsum(lengths_row)
    place = jnp.arange(rows_tok, dtype=jnp.int32)
    segment = jnp.sum((place[:, None] >= ends[None, :]).astype(jnp.int32), axis=1)
    starts = jnp.concatenate([ends - lengths_row, ends[-1:]])
    labels = jnp.arange(starts.shape[0], dtype=jnp.int32)
    begin = jnp.sum(jnp.where(segment[:, None] == labels[None, :], starts[None, :], 0), axis=1)
    position = (place - begin).astype(F32)
    valid = segment < lengths_row.shape[0]
    label_tok = jnp.where(valid, segment, lengths_row.shape[0] + place)
    allowed = (label_tok[:, None] == label_tok[None, :]) & (place[None, :] <= place[:, None])
    return (position, valid, allowed)


def turn_tables(position):
    half = ROT // 2
    freq = jnp.exp(jnp.arange(half, dtype=F32) * (-2.0 * math.log(10000.0) / ROT))
    turn = position.reshape(-1)[:, None] * freq[None, :]
    cosine, sine = jnp.cos(turn), jnp.sin(turn)
    rest = (turn.shape[0], HD - ROT)
    cos_t = jnp.concatenate([cosine, cosine, jnp.ones(rest, F32)], axis=1)
    sin_t = jnp.concatenate([-sine, sine, jnp.zeros(rest, F32)], axis=1)
    return (jnp.tile(cos_t, (1, 2)), jnp.tile(sin_t, (1, 2)))


def turned(v, cos_t, sin_t, low_half):
    partner = jnp.where(low_half, pltpu.roll(v, TILE - ROT // 2, 1), pltpu.roll(v, ROT // 2, 1))
    return v * cos_t + partner * sin_t

def stacked(v, first):
    zero = jnp.zeros_like(v)
    return jnp.concatenate([jnp.where(first, v, zero), jnp.where(first, zero, v)], axis=0)

def softmax_of(query2, keys, bias2):
    scores = lax.dot_general(query2, keys, (((1,), (1,)), ((), ())), preferred_element_type=F32)
    scores = scores * 0.125 + bias2
    lifted = jnp.exp(scores - jnp.max(scores, axis=1, keepdims=True))
    return lifted / jnp.sum(lifted, axis=1, keepdims=True)

def forward_kernel(cols, main, rest, proj_ref, bqkv_ref, cos_ref, sin_ref, mask_ref, joined_ref, qkv_ref):
    rows = proj_ref.shape[0]
    lane = lax.broadcasted_iota(jnp.int32, (rows, TILE), 1)
    first = lane < HD
    low_half = lane % HD < ROT // 2
    cos_t, sin_t = cos_ref[...], sin_ref[...]
    bias2 = jnp.concatenate([mask_ref[0], mask_ref[0]], axis=0)
    for pair in range(cols // TILE):
        at = [g * cols + pair * TILE for g in range(3)]
        query, keys, values = (
            proj_ref[:, a : a + TILE] + bqkv_ref[0:1, a : a + TILE] for a in at
        )
        query = turned(query, cos_t, sin_t, low_half).astype(BF)
        keys = turned(keys, cos_t, sin_t, low_half).astype(BF)
        values = values.astype(BF)
        for a, v in zip(at, (query, keys, values)):
            qkv_ref[:, a : a + TILE] = v
        probs = softmax_of(stacked(query, first), keys, bias2).astype(BF)
        mixed = jnp.dot(probs, values, preferred_element_type=F32)
        joined_ref[:, pair * TILE : (pair + 1) * TILE] = jnp.where(
            first, mixed[:rows], mixed[rows:]
        ).astype(BF)
    base = 3 * cols
    for j in range(main // TILE):
        gate = proj_ref[:, base + j * TILE : base + (j + 1) * TILE]
        up = proj_ref[:, base + main + j * TILE : base + main + (j + 1) * TILE]
        hid = gate * jax.nn.sigmoid(gate) * up
        joined_ref[:, cols + j * TILE : cols + (j + 1) * TILE] = hid.astype(BF)
    if rest:
        tail = proj_ref[:, base + 2 * main :]
        up = pltpu.roll(tail, rest, 1)
        hid = tail * jax.nn.sigmoid(tail) * up
        joined_ref[:, cols + main :] = hid[:, :rest].astype(BF)

def backward_kernel(cols, main, rest, proj_ref, back_ref, qkv_ref, cos_ref, sin_ref, mask_ref, grad_ref, sum_ref):
    rows = proj_ref.shape[0]
    lane = lax.broadcasted_iota(jnp.int32, (rows, TILE), 1)
    first = lane < HD
    low_half = lane % HD < ROT // 2
    cos_t, sin_t = cos_ref[...], sin_ref[...]
    bias2 = jnp.concatenate([mask_ref[0], mask_ref[0]], axis=0)

    @pl.when(pl.program_id(0) == 0)
    def _():
        sum_ref[...] = jnp.zeros_like(sum_ref)

    across = (((0,), (0,)), ((), ()))
    for pair in range(cols // TILE):
        at = [g * cols + pair * TILE for g in range(3)]
        query, keys, values = (qkv_ref[:, a : a + TILE] for a in at)
        query2 = stacked(query, first)
        mixed2 = stacked(back_ref[:, pair * TILE : (pair + 1) * TILE].astype(BF), first)
        probs = softmax_of(query2, keys, bias2)
        grad_probs = lax.dot_general(
            mixed2, values, (((1,), (1,)), ((), ())), preferred_element_type=F32
        )
        inner = jnp.sum(probs * grad_probs, axis=1, keepdims=True)
        grad_scores = (probs * (grad_probs - inner)).astype(BF)
        gq = jnp.dot(grad_scores, keys, preferred_element_type=F32)
        gq = jnp.where(first, gq[:rows], gq[rows:]) * 0.125
        gk = lax.dot_general(grad_scores, query2, across, preferred_element_type=F32) * 0.125
        gv = lax.dot_general(probs.astype(BF), mixed2, across, preferred_element_type=F32)
        gq = turned(gq, cos_t, -sin_t, low_half)
        gk = turned(gk, cos_t, -sin_t, low_half)
        for a, v in zip(at, (gq, gk, gv)):
            low = v.astype(BF)
            grad_ref[:, a : a + TILE] = low
            sum_ref[0:1, a : a + TILE] += jnp.sum(low.astype(F32), axis=0, keepdims=True)
    base = 3 * cols

    def gates(gate, up, grad_hid):
        sigma = jax.nn.sigmoid(gate)
        slope = sigma * (1.0 + gate * (1.0 - sigma))
        return (grad_hid * up * slope, grad_hid * (gate * sigma))

    for j in range(main // TILE):
        a, b = base + j * TILE, base + main + j * TILE
        gate, up = proj_ref[:, a : a + TILE], proj_ref[:, b : b + TILE]
        grad_hid = back_ref[:, cols + j * TILE : cols + (j + 1) * TILE]
        gg, gu = gates(gate, up, grad_hid)
        grad_ref[:, a : a + TILE] = gg.astype(BF)
        grad_ref[:, b : b + TILE] = gu.astype(BF)
    if rest:
        tail = proj_ref[:, base + 2 * main :]
        short = back_ref[:, cols + main :]
        grad_hid = jnp.concatenate([short, jnp.zeros_like(short)], axis=1)
        gg, gu = gates(tail, pltpu.roll(tail, rest, 1), grad_hid)
        both = jnp.where(lane < rest, gg, pltpu.roll(gu, rest, 1))
        grad_ref[:, base + 2 * main :] = both.astype(BF)

def forward_call(proj, bqkv, cos_t, sin_t, mask, cols, main, rest, rows):
    n = proj.shape[0] // rows
    row = lambda w: pl.BlockSpec((rows, w), lambda i: (i, 0))
    return pl.pallas_call(
        functools.partial(forward_kernel, cols, main, rest),
        grid=(n,),
        in_specs=[row(proj.shape[1]), pl.BlockSpec((8, 3 * cols), lambda i: (0, 0)), row(TILE), row(TILE),
                  pl.BlockSpec((1, rows, rows), lambda i: (i, 0, 0))],
        out_specs=[row(cols + main + rest), row(3 * cols)],
        out_shape=[jax.ShapeDtypeStruct((proj.shape[0], cols + main + rest), BF), jax.ShapeDtypeStruct((proj.shape[0], 3 * cols), BF)],
        compiler_params=pltpu.CompilerParams(dimension_semantics=("arbitrary",), vmem_limit_bytes=32 << 20),
        name="attend",
    )(proj, bqkv, cos_t, sin_t, mask)

def backward_call(proj, back, qkv, cos_t, sin_t, mask, cols, main, rest, rows):
    n = proj.shape[0] // rows
    row = lambda w: pl.BlockSpec((rows, w), lambda i: (i, 0))
    return pl.pallas_call(
        functools.partial(backward_kernel, cols, main, rest),
        grid=(n,),
        in_specs=[row(proj.shape[1]), row(back.shape[1]), row(3 * cols), row(TILE), row(TILE),
                  pl.BlockSpec((1, rows, rows), lambda i: (i, 0, 0))],
        out_specs=[row(proj.shape[1]), pl.BlockSpec((8, 3 * cols), lambda i: (0, 0))],
        out_shape=[jax.ShapeDtypeStruct(proj.shape, BF), jax.ShapeDtypeStruct((8, 3 * cols), F32)],
        compiler_params=pltpu.CompilerParams(dimension_semantics=("arbitrary",), vmem_limit_bytes=32 << 20),
        name="attend_back",
    )(proj, back, qkv, cos_t, sin_t, mask)


def column_plan(member, outer, wide, cores, own, own_ff, cols, main, rest):
    z, c = member // cores, member % cores
    out = []
    for g in range(3):
        for k in range(wide):
            out.append((0, ((g * outer + z) * wide + k) * cores * own + c * own, g * cols + k * own, own))
    for which in range(2):
        for k in range(wide):
            src = ((z * wide + k) * cores + c) * own_ff
            lo, hi = k * own_ff, (k + 1) * own_ff
            cut = min(hi, main)
            if cut > lo:
                out.append((1 + which, src, 3 * cols + which * main + lo, cut - lo))
            low = max(lo, main)
            if hi > low:
                out.append((1 + which, src + low - lo, 3 * cols + 2 * main + which * rest + low - main, hi - low))
    return out

def pack_kernel(plan, tp, member_ref, qkv_ref, gate_ref, up_ref, *refs):
    outs, slots, sem = refs[:tp], refs[tp], refs[tp + 1]
    member = member_ref[0]
    arrays = (qkv_ref, gate_ref, up_ref)
    for t in range(tp):
        for which, src, dst, width in plan(t):
            slots[t, :, dst : dst + width] = arrays[which][:, src : src + width]
    copies = [
        pltpu.make_async_copy(slots.at[lax.bitwise_xor(member, r)], outs[r], sem.at[r]) for r in range(tp)
    ]
    for copy in copies:
        copy.start()
    for copy in copies:
        copy.wait()

def pack_call(member, w_qkv, w_gate, w_up, plan, tp, total):
    own = w_qkv.shape[0]
    return pl.pallas_call(
        functools.partial(pack_kernel, plan, tp),
        in_specs=[pl.BlockSpec(memory_space=pltpu.SMEM)] + [pl.BlockSpec(memory_space=pltpu.VMEM)] * 3,
        out_specs=[pl.BlockSpec(memory_space=pl.ANY)] * tp,
        out_shape=[jax.ShapeDtypeStruct((own, total), BF)] * tp,
        scratch_shapes=[pltpu.VMEM((tp, own, total), BF), pltpu.SemaphoreType.DMA((tp,))],
        compiler_params=pltpu.CompilerParams(vmem_limit_bytes=32 << 20),
        name="pack_columns",
    )(member, w_qkv, w_gate, w_up)

def unpack_kernel(plan, tp, member_ref, *refs):
    ins, outs, slots, sem = refs[:tp], refs[tp : tp + 3], refs[tp + 3], refs[tp + 4]
    member = member_ref[0]
    copies = [
        pltpu.make_async_copy(ins[r], slots.at[lax.bitwise_xor(member, r)], sem.at[r]) for r in range(tp)
    ]
    for copy in copies:
        copy.start()
    for copy in copies:
        copy.wait()
    for t in range(tp):
        for which, src, dst, width in plan(t):
            outs[which][:, src : src + width] = slots[t, :, dst : dst + width].astype(F32)

def unpack_call(member, parts, plan, widths):
    tp = len(parts)
    own, total = parts[0].shape
    return pl.pallas_call(
        functools.partial(unpack_kernel, plan, tp),
        in_specs=[pl.BlockSpec(memory_space=pltpu.SMEM)] + [pl.BlockSpec(memory_space=pl.ANY)] * tp,
        out_specs=[pl.BlockSpec(memory_space=pltpu.VMEM)] * 3,
        out_shape=[jax.ShapeDtypeStruct((own, w), F32) for w in widths],
        scratch_shapes=[pltpu.VMEM((tp, own, total), BF), pltpu.SemaphoreType.DMA((tp,))],
        compiler_params=pltpu.CompilerParams(vmem_limit_bytes=32 << 20),
        name="unpack_columns",
    )(member, *parts)


def move_all(pairs_of, *args):
    pairs = pairs_of(*args)
    for when, src, dst, sem in pairs:
        copy = pltpu.make_async_copy(src, dst, sem)
        if when is None:
            copy.start()
        else:
            pl.when(when)(copy.start)
    for when, src, dst, sem in pairs:
        copy = pltpu.make_async_copy(src, dst, sem)
        if when is None:
            copy.wait()
        else:
            pl.when(when)(copy.wait)


def mover(pairs_of, index, arrays, shapes, copies, name):
    count = len(arrays)

    def kernel(index_ref, *refs):
        move_all(pairs_of, index_ref[0], refs[:count], refs[count:-1], refs[-1])

    anywhere = pl.BlockSpec(memory_space=pl.ANY)
    return pl.pallas_call(
        kernel,
        in_specs=[pl.BlockSpec(memory_space=pltpu.SMEM)] + [anywhere] * count,
        out_specs=[anywhere] * len(shapes),
        out_shape=[jax.ShapeDtypeStruct(shape, BF) for shape in shapes],
        scratch_shapes=[pltpu.SemaphoreType.DMA((copies,))],
        name=name,
    )(index, *arrays)


def stack_call(member, parts):
    tp = len(parts)
    rows, width = parts[0].shape
    half = tp // 2

    def pairs(me, ins, outs, sem):
        out = []
        for r in range(tp):
            spot = lax.bitwise_xor(me, r)
            for h in range(2):
                at = pl.multiple_of((spot - h * half) * rows, rows)
                dst = outs[h].at[pl.ds(at, rows), :]
                out.append((spot // half == h, ins[r], dst, sem.at[r]))
        return out

    return mover(pairs, member, parts, [(half * rows, width)] * 2, tp, "stack_rows")


def cut_call(member, low, high, tp):
    half = tp // 2
    rows = low.shape[0] // half
    width = low.shape[1]

    def pairs(me, ins, outs, sem):
        out = []
        for r in range(tp):
            spot = lax.bitwise_xor(me, r)
            for h in range(2):
                at = pl.multiple_of((spot - h * half) * rows, rows)
                src = ins[h].at[pl.ds(at, rows), :]
                out.append((spot // half == h, src, outs[r], sem.at[r]))
        return out

    return mover(pairs, member, [low, high], [(rows, width)] * tp, tp, "cut_rows")


def row_pairs(me, wide, own, own_ff, cut, halves, whole, sem, inward):
    out = []
    for j in range(wide):
        spot = lax.bitwise_xor(me, j)
        base = wide * own
        spans = (
            (0, 0, pl.multiple_of(base + spot * own_ff, 16), cut),
            (1, 0, pl.multiple_of(spot * own, 16), own),
            (1, own, pl.multiple_of(base + spot * own_ff + cut, 16), own_ff - cut),
        )
        for i, (h, at, place, size) in enumerate(spans):
            here = halves[2 * j + h].at[pl.ds(at, size), :]
            there = whole.at[pl.ds(place, size), :]
            src, dst = (here, there) if inward else (there, here)
            out.append((None, src, dst, sem.at[3 * j + i]))
    return out


def place_call(lane, blocks, own, own_ff):
    wide = len(blocks)
    cut, width = blocks[0][0].shape
    arrays = [half for pair in blocks for half in pair]

    def pairs(me, ins, outs, sem):
        return row_pairs(me, wide, own, own_ff, cut, ins, outs[0], sem, True)

    shape = (wide * (own + own_ff), width)
    return mover(pairs, lane, arrays, [shape], 3 * wide, "place_rows")[0]


def pick_call(lane, part, wide, own, own_ff, cut):
    width = part.shape[1]

    def pairs(me, ins, outs, sem):
        return row_pairs(me, wide, own, own_ff, cut, outs, ins[0], sem, False)

    shapes = [(cut, width), (own + own_ff - cut, width)] * wide
    outs = mover(pairs, lane, [part], shapes, 3 * wide, "pick_rows")
    return [outs[2 * j : 2 * j + 2] for j in range(wide)]


class Plain:
    def __init__(self, outer, inner):
        self.tp, self.wide, self.cores, self.outer = outer, inner, 1, outer
        self.member = lax.axis_index("dp")
        self.lane = lax.axis_index("fsdp")

    def group_lengths(self, lengths):
        return lax.all_gather(lengths, "dp", axis=0, tiled=True)

    def gather_tokens(self, block):
        return lax.all_gather(block, "dp", axis=0, tiled=True)

    def scatter_tokens(self, lhs, rhs, dims):
        part = lax.dot_general(lhs, rhs, dims, preferred_element_type=F32).astype(BF)
        return lax.psum_scatter(part, "dp", scatter_dimension=0, tiled=True).astype(F32)

    def columns_in(self, arrays, plan, total):
        own = arrays[0].shape[0]
        packed = []
        for member in range(self.tp):
            pieces = sorted(plan(member), key=lambda item: item[2])
            packed.append(jnp.concatenate([arrays[i][:, s : s + w] for i, s, _, w in pieces], 1))
        got = lax.all_to_all(jnp.stack(packed), "dp", split_axis=0, concat_axis=0, tiled=True)
        got = got.reshape(self.tp * own, total)
        return lax.all_gather(got, "fsdp", axis=0, tiled=True)

    def columns_out(self, lhs, rhs, plan, widths):
        part = lax.dot_general(lhs, rhs, CONTRACT_ROWS, preferred_element_type=F32).astype(BF)
        part = lax.psum_scatter(part, "fsdp", scatter_dimension=0, tiled=True)
        part = part.reshape(self.tp, -1, part.shape[1])
        got = lax.all_to_all(part, "dp", split_axis=0, concat_axis=0, tiled=True)
        outs = []
        for which, width in enumerate(widths):
            pieces = [(s, m, d, w) for m in range(self.tp) for i, s, d, w in plan(m) if i == which]
            outs.append(jnp.concatenate([got[m][:, d : d + w] for s, m, d, w in sorted(pieces)], 1))
        return [out.astype(F32) for out in outs]

    def rows_in(self, w_out, w_down):
        return jnp.concatenate(
            [lax.all_gather(w, "fsdp", axis=0, tiled=True) for w in (w_out, w_down)], axis=0
        )

    def rows_out(self, part, own, own_ff):
        cols = self.wide * own
        return [
            lax.psum_scatter(p, "fsdp", scatter_dimension=0, tiled=True).astype(F32)
            for p in (part[:cols], part[cols:])
        ]

    def relative(self, blocks, axis):
        return blocks

    def scatter_stats(self, stats):
        return lax.psum_scatter(stats, AXES, scatter_dimension=0, tiled=True)[0]


class Linked:
    def __init__(self, outer, inner):
        self.outer, self.cores, self.wide = outer, 2, inner // 2
        self.tp = outer * 2
        flat = lax.axis_index("fsdp")
        self.core = lax.rem(flat, 2)
        self.lane = flat // 2
        self.depth = lax.axis_index("dp")
        self.member = self.depth * 2 + self.core

    def send(self, value, dz=0, dk=0, dc=0):
        pairs = []
        for z in range(self.outer):
            for k in range(self.wide):
                for c in range(2):
                    here = (z * self.wide + k) * 2 + c
                    pairs.append((here, ((z ^ dz) * self.wide + (k ^ dk)) * 2 + (c ^ dc)))
        return lax.ppermute(value, AXES, pairs)

    def group_lengths(self, lengths):
        return self.gather_tokens(lengths)

    def gather_tokens(self, block):
        parts = [block] + [self.send(block, dz=dz) for dz in range(1, self.outer)]
        mine = jnp.concatenate(parts, axis=0)
        return jnp.concatenate([mine, self.send(mine, dc=1)], axis=0)

    def scatter_tokens(self, lhs, rhs, dims):
        half = lhs.shape[0] // 2
        far = lax.dot_general(lhs[half:], rhs, dims, preferred_element_type=F32).astype(BF)
        got = self.send(far, dc=1)
        near = lax.dot_general(lhs[:half], rhs, dims, preferred_element_type=F32)
        rows = half // self.outer
        chip = near + got.astype(F32)
        total = chip[:rows]
        for dz in range(1, self.outer):
            piece = chip[dz * rows : (dz + 1) * rows].astype(BF)
            total = total + self.send(piece, dz=dz).astype(F32)
        return total

    def exchange(self, parts):
        return [parts[0]] + [
            self.send(parts[step], dz=step // 2, dc=step % 2) for step in range(1, self.tp)
        ]

    def index(self):
        return self.member.astype(jnp.int32).reshape(1)

    def columns_in(self, arrays, plan, total):
        parts = self.exchange(pack_call(self.index(), *arrays, plan, self.tp, total))
        halves = stack_call(self.index(), parts)
        from_x = [self.send(half, dk=1) for half in halves]
        from_y = [self.send(half, dk=2) for half in halves]
        last = [self.send(from_x[0], dk=2), self.send(from_y[1], dk=1)]
        return jnp.concatenate([*halves, *from_x, *from_y, *last], axis=0)

    def sum_halves(self, blocks):
        low = self.send(blocks[3][0], dk=1)
        high = self.send(blocks[3][1], dk=2)
        x_low = self.send(blocks[1][0], dk=1)
        y_high = self.send(blocks[2][1], dk=2)
        x_high = self.send((blocks[1][1].astype(F32) + high.astype(F32)).astype(BF), dk=1)
        y_low = self.send((blocks[2][0].astype(F32) + low.astype(F32)).astype(BF), dk=2)
        return [
            (blocks[0][0].astype(F32) + x_low.astype(F32) + y_low.astype(F32)),
            (blocks[0][1].astype(F32) + x_high.astype(F32) + y_high.astype(F32)),
        ]

    def columns_out(self, lhs, rhs, plan, widths):
        size = lhs.shape[1] // self.wide // 2
        blocks = [[None, None] for _ in range(self.wide)]
        for j, h in ((3, 0), (3, 1), (1, 0), (2, 1), (1, 1), (2, 0), (0, 0), (0, 1)):
            at = (2 * j + h) * size
            blocks[j][h] = lax.dot_general(
                lhs[:, at : at + size], rhs, CONTRACT_ROWS, preferred_element_type=F32
            ).astype(BF)
        low, high = self.sum_halves(blocks)
        parts = cut_call(self.index(), low.astype(BF), high.astype(BF), self.tp)
        return unpack_call(self.index(), self.exchange(parts), plan, widths)

    def rows_in(self, w_out, w_down):
        cut = w_down.shape[0] // 32 * 16 + 32
        halves = [w_down[:cut], jnp.concatenate([w_out, w_down[cut:]], axis=0)]
        from_x = [self.send(half, dk=1) for half in halves]
        from_y = [self.send(half, dk=2) for half in halves]
        last = [self.send(from_x[0], dk=2), self.send(from_y[1], dk=1)]
        lane = self.lane.astype(jnp.int32).reshape(1)
        return place_call(lane, [halves, from_x, from_y, last], w_out.shape[0], w_down.shape[0])

    def rows_out(self, part, own, own_ff):
        cut = own_ff // 32 * 16 + 32
        lane = self.lane.astype(jnp.int32).reshape(1)
        low, high = self.sum_halves(pick_call(lane, part, self.wide, own, own_ff, cut))
        return [high[:own], jnp.concatenate([low, high[own:]], axis=0)]

    def relative(self, blocks, axis):
        shape = blocks.shape
        split = blocks.reshape(shape[:axis] + (2, 2) + shape[axis + 1 :])
        split = jnp.where(self.lane >= 2, jnp.flip(split, axis), split)
        split = jnp.where(lax.rem(self.lane, 2) == 1, jnp.flip(split, axis + 1), split)
        return split.reshape(shape)

    def scatter_stats(self, stats):
        width = stats.shape[1]
        split = stats.reshape(self.outer, self.wide, 2, width)

        def keep(values, axis, place, count, name):
            total = lax.dynamic_index_in_dim(values, place, axis, keepdims=False)
            for step in range(1, count):
                spot = lax.bitwise_xor(place, step)
                piece = lax.dynamic_index_in_dim(values, spot, axis, keepdims=False)
                total = total + self.send(piece, **{name: step})
            return total

        split = keep(split, 2, self.core, 2, "dc")
        split = keep(split, 1, self.lane, self.wide, "dk")
        return keep(split, 0, self.depth, self.outer, "dz")


def on_device(
    tokens, ln_gain, ln_shift, w_qkv, b_qkv, w_out, w_gate, w_up, w_down, grad_out, seq_lengths
):
    outer, inner = lax.axis_size("dp"), lax.axis_size("fsdp")
    linked = outer == 4 and inner == 8
    net = Linked(outer, inner) if linked else Plain(outer, inner)
    tp, wide, cores = net.tp, net.wide, net.cores
    rows_tok, width = tokens.shape
    own = w_qkv.shape[0]
    own_ff = w_down.shape[0]
    cols, cols_ff = wide * own, wide * own_ff
    main = cols_ff // TILE * TILE
    rest = cols_ff - main
    total = 3 * cols + 2 * cols_ff
    plan = lambda member: column_plan(
        member, outer, wide, cores, own, own_ff, cols, main, rest
    )

    _, valid, _ = block_terms(seq_lengths[0], rows_tok)
    keep_row = valid.astype(F32)[:, None]
    widened = tokens.astype(F32)
    centered = widened - jnp.mean(widened, axis=1, keepdims=True)
    inv_std = lax.rsqrt(jnp.mean(centered * centered, axis=1, keepdims=True) + EPS)
    scaled = centered * inv_std
    normed = (scaled * ln_gain + ln_shift).astype(BF)
    masked = (grad_out.astype(F32) * keep_row).astype(BF)

    def lanes_first(x):
        split = x.reshape(rows_tok, outer, wide, cores * own)
        return net.relative(jnp.swapaxes(split, 1, 2), 1).reshape(rows_tok, width)

    def lanes_back(x):
        split = net.relative(x.reshape(rows_tok, wide, outer, cores * own), 1)
        return jnp.swapaxes(split, 1, 2).reshape(rows_tok, width)

    entry = net.columns_in([w_qkv, w_gate, w_up], plan, total)
    mixer = net.rows_in(w_out, w_down)
    lengths = net.group_lengths(seq_lengths)
    normed_all = net.gather_tokens(lanes_first(normed))
    masked_all = net.gather_tokens(masked)
    position, _, allowed = jax.vmap(lambda row: block_terms(row, rows_tok))(lengths)
    cos_t, sin_t = turn_tables(position)
    mask = jnp.where(allowed, 0.0, NEG)
    bias = lax.dynamic_index_in_dim(
        jnp.transpose(b_qkv.reshape(3, outer, wide, cores, own), (1, 3, 0, 2, 4)).reshape(tp, -1),
        net.member,
        0,
    )
    bias = jnp.broadcast_to(bias, (8, 3 * cols))

    proj = jnp.dot(normed_all, entry, preferred_element_type=F32)
    joined, qkv = forward_call(proj, bias, cos_t, sin_t, mask, cols, main, rest, rows_tok)
    branch = net.scatter_tokens(joined, mixer, (((1,), (0,)), ((), ())))
    output = (widened + keep_row * branch).astype(BF)

    back = lax.dot_general(masked_all, mixer, CONTRACT_COLS, preferred_element_type=F32)
    grad_entry, bias_part = backward_call(
        proj, back, qkv, cos_t, sin_t, mask, cols, main, rest, rows_tok
    )
    grad_w_qkv, grad_w_gate, grad_w_up = net.columns_out(
        normed_all, grad_entry, plan, (w_qkv.shape[1], w_gate.shape[1], w_up.shape[1])
    )
    mixer_part = lax.dot_general(
        joined, masked_all, CONTRACT_ROWS, preferred_element_type=F32
    ).astype(BF)
    grad_w_out, grad_w_down = net.rows_out(mixer_part, own, own_ff)

    grad_norm = lanes_back(net.scatter_tokens(grad_entry, entry, CONTRACT_COLS))
    lifted_grad = grad_norm * ln_gain
    grad_in = inv_std * (
        lifted_grad
        - jnp.mean(lifted_grad, axis=1, keepdims=True)
        - scaled * jnp.mean(lifted_grad * scaled, axis=1, keepdims=True)
    )
    grad_tokens = (grad_out.astype(F32) + grad_in).astype(BF)

    shards = outer * inner
    gain_part = jnp.sum(grad_norm * scaled, axis=0)
    shift_part = jnp.sum(grad_norm, axis=0)
    bias_full = lax.dynamic_update_index_in_dim(
        jnp.zeros((tp, 3 * cols), F32), bias_part[0], net.member, 0
    )
    bias_full = jnp.transpose(bias_full.reshape(outer, cores, 3, wide, own), (2, 0, 3, 1, 4))
    stats = jnp.concatenate(
        [
            gain_part.reshape(shards, own),
            shift_part.reshape(shards, own),
            bias_full.reshape(shards, 3 * own),
        ],
        axis=1,
    )
    stats = net.scatter_stats(stats)
    return (
        output,
        grad_tokens,
        grad_w_qkv,
        grad_w_out,
        grad_w_gate,
        grad_w_up,
        grad_w_down,
        stats[:own],
        stats[own : 2 * own],
        stats[2 * own :],
    )


def solution(mesh):
    rows = P(AXES, None)
    return jax.shard_map(
        on_device,
        mesh=mesh,
        in_specs=(rows, P(), P(), rows, P(), rows, rows, rows, rows, rows, rows),
        out_specs=(rows,) * 7 + (P(AXES),) * 3,
        check_vma=False,
    )
```

time: 700 us -> 905 us (1.29)
  Pallas kernels: 0 us -> 401 us
  waiting for transfers between devices: 283 us -> 179 us
  starting transfers between devices: 48.4 us -> 145 us
  blocking collectives: 86.7 us -> 0 us
  local copies, waits for them, and re-layouts: 138 us -> 54.6 us
  other arithmetic: 63.9 us -> 30.6 us
  matrix products: 67.7 us -> 82.6 us
    pallas_call x0 -> x8, Pallas kernels: none -> 401 us  [the longest x4 378 us: mover(): pl.pallas_call(kernel, in_specs=[pl.BlockSpec(memory_space=pltpu.SMEM)] +...]
    ppermute x50 -> x65, waiting for transfers between devices: 283 us -> 179 us  [send(): return lax.ppermute(value, AXES, pairs)]
    ppermute x50 -> x65, starting transfers between devices: 48.4 us -> 145 us  [send(): return lax.ppermute(value, AXES, pairs)]
    reshape x23 -> x0, local copies, waits for them, and re-layouts: 54 us -> none  [the longest x6 19 us: unpack(): split = part.reshape(outer, cores, own, groups, wide, piece)]
    all_gather x1 -> x0, blocking collectives: 46.4 us -> none  [on_device(): lax.all_gather(seq_lengths, AXES, axis=0, tiled=True)]
    unnamed x1 -> x0, blocking collectives: 40.3 us -> none
    convert_element_type x7 -> x2, other arithmetic: 16.8 us -> 1.01 us  [the longest x1 0.88 us: sum_halves(): (blocks[2][0].astype(F32) + low.astype(F32)).astype(BF)]
    another operation x11 -> x1, other arithmetic: 15.6 us -> 0.83 us
  transfers between devices with their start and end apart: 50 -> 65, of which waited for: 21 -> 18; matrix products, arithmetic and copies ran while one was open for 17% -> 13% of each run, Pallas kernels for 0% -> 29%
where the time goes in v2:
time: 905 us; the launch traced here: 894 us
  Pallas kernels  401 us (44%)
  waiting for transfers between devices  179 us (20%)
  starting transfers between devices  145 us (16%)
  matrix products  82.6 us (9%)
  local copies, waits for them, and re-layouts  54.6 us (6%)
  other arithmetic  30.6 us (3%)
    pallas_call x4, Pallas kernels, mover(): pl.pallas_call(kernel, in_specs=[pl.BlockSpec(memory_space=pltpu.SMEM)] +...  378 us
    ppermute x65, waiting for transfers between devices, send(): return lax.ppermute(value, AXES, pairs)  179 us
    ppermute x65, starting transfers between devices, send(): return lax.ppermute(value, AXES, pairs)  145 us
    unnamed x104, local copies, waits for them, and re-layouts  31.6 us
    dot_general x8, matrix products, columns_out(): lax.dot_general(lhs[:, at:at + size], rhs, CONTRACT_ROWS, preferred_eleme...  27.8 us
  transfers between devices with their start and end apart: 65, of which 18 were waited for; matrix products, arithmetic and copies ran while one was open for 13% of the time, Pallas kernels for 29%

profile of v2, /device:TPU:0, one launch (start us, length us, event | category | flops | bytes accessed | tf_op | source)
XLA Modules:
  0.0 894.5 jit_solution(3508866271792486170)
XLA Ops:
  49.2 20.8 %collective-permute-done.8.refs_5_ = bf16[64,2176]{1,0:T(8,128)(2,1)} collective-permute-done((bf16[64,2176]{1,0:T(8,128)(2,1)S(1)}, bf16[64,2176]{1,0:T(8,128)(2,1)}, u32[]{:S(2)}, u32[]{:S(2)}) %collective-permute-start.8) | collective-permute-done | bytes 278560 | tf_op jit(solution)/shard_map/ppermute | solution.py:437
  73.7 17.6 %collective-permute-start.1 = (bf16[128,2048]{1,0:T(8,128)(2,1)}, bf16[128,2048]{1,0:T(8,128)(2,1)}, u32[]{:S(2)}, u32[]{:S(2)}) collective-permute-start(bf16[128,2048]{1,0:T(8,128)(2,1)} %copy-done.11), channel_id=1, source_target_pairs={{0,16},{1,17},{2,18},{3,19},{4,20},{5,21},{6,22},{7,23},{8,24},{9,... | collective-permute-start | bytes 1572872 | tf_op jit(solution)/shard_map/ppermute | solution.py:437
  91.3 15.2 %collective-permute-start = (bf16[128,2048]{1,0:T(8,128)(2,1)}, bf16[128,2048]{1,0:T(8,128)(2,1)}, u32[]{:S(2)}, u32[]{:S(2)}) collective-permute-start(bf16[128,2048]{1,0:T(8,128)(2,1)} %copy-done.11), channel_id=1, source_target_pairs={{0,8},{1,9},{2,10},{3,11},{4,12},{5,13},{6,14},{7,15},{8,0},{9,1},... | collective-permute-start | bytes 1572872 | tf_op jit(solution)/shard_map/ppermute | solution.py:437
  106.5 68.7 %stack_rows.1 = (bf16[256,2176]{1,0:T(8,128)(2,1)}, bf16[256,2176]{1,0:T(8,128)(2,1)}) custom-call(s32[1]{0:T(128)} %bitcast.5.member_ref.index_ref, bf16[64,2176]{1,0:T(8,128)(2,1)} %copy-done.5, bf16[64,2176]{1,0:T(8,128)(2,1)} %collective-permute-done.4.refs_1_, bf16[64,2176]{1,0:T(8,128)(2,1)} %collective-permute-done.5.refs_2_, ...), custom_call_target="tpu_custom_call" | custom-call | tf_op jit(solution)/shard_map/stack_rows/pallas_call | solution.py:277
  199.6 9.5 %collective-permute-done.33 = bf16[128,2048]{1,0:T(8,128)(2,1)S(1)} collective-permute-done((bf16[128,2048]{1,0:T(8,128)(2,1)S(1)}, bf16[128,2048]{1,0:T(8,128)(2,1)S(1)}, u32[]{:S(2)}, u32[]{:S(2)}) %collective-permute-start.33) | collective-permute-done | bytes 524320 | tf_op jit(solution)/shard_map/ppermute | solution.py:437
  209.6 26.6 %collective-permute-done.32 = bf16[128,2048]{1,0:T(8,128)(2,1)S(1)} collective-permute-done((bf16[128,2048]{1,0:T(8,128)(2,1)S(1)}, bf16[128,2048]{1,0:T(8,128)(2,1)S(1)}, u32[]{:S(2)}, u32[]{:S(2)}) %collective-permute-start.32) | collective-permute-done | bytes 524320 | tf_op jit(solution)/shard_map/ppermute | solution.py:437
  240.5 13.4 %collective-permute-done.26.refs_7_ = bf16[128,2048]{1,0:T(8,128)(2,1)S(1)} collective-permute-done((bf16[128,2048]{1,0:T(8,128)(2,1)S(1)}, bf16[128,2048]{1,0:T(8,128)(2,1)S(1)}, u32[]{:S(2)}, u32[]{:S(2)}) %collective-permute-start.26) | collective-permute-done | bytes 524320 | tf_op jit(solution)/shard_map/ppermute | solution.py:437
  254.7 120.3 %place_rows.1 = bf16[960,2048]{1,0:T(8,128)(2,1)} custom-call(s32[1]{0:T(128)} %bitcast.10.index_ref, bf16[112,2048]{1,0:T(8,128)(2,1)} %slice.95.refs_0_, bf16[128,2048]{1,0:T(8,128)(2,1)} %pad_maximum_fusion.3.refs_1_, bf16[112,2048]{1,0:T(8,128)(2,1)} %collective-permute-done.21.refs_2_, bf16[128,2048]{1,0:T(8,128)(2,1)} %copy-done.19, ...), custom_call_target="tpu_custom_call" | custom-call | tf_op jit(solution)/shard_map/place_rows/pallas_call | solution.py:277
  387.4 17.2 %collective-permute-done.15 = bf16[256,2176]{1,0:T(8,128)(2,1)S(1)} collective-permute-done((bf16[256,2176]{1,0:T(8,128)(2,1)}, bf16[256,2176]{1,0:T(8,128)(2,1)S(1)}, u32[]{:S(2)}, u32[]{:S(2)}) %collective-permute-start.15) | collective-permute-done | bytes 1114144 | tf_op jit(solution)/shard_map/ppermute | solution.py:437
  414.8 14.5 %fusion.62.proj_ref = f32[1024,2176]{1,0:T(8,128)S(1)} fusion(bf16[1024,2048]{1,0:T(8,128)(2,1)} %constant_dynamic-update-slice_fusion, bf16[2048,2176]{1,0:T(8,128)(2,1)} %constant_dynamic-update-slice_fusion.5), kind=kOutput, calls=%fused_computation.154 | convolution fusion | flops 9126805504 | bytes 22020096 | tf_op jit(solution)/shard_map/dot_general | solution.py:589
  429.3 7.3 attend.1
  436.6 11.0 %attend_back.1 = (bf16[1024,2176]{1,0:T(8,128)(2,1)S(1)}, f32[8,768]{1,0:T(8,128)S(1)}) custom-call(f32[1024,2176]{1,0:T(8,128)S(1)} %fusion.62.proj_ref, f32[1024,960]{1,0:T(8,128)S(1)} %fusion.63.back_ref, bf16[1024,768]{1,0:T(8,128)(2,1)S(1)} %get-tuple-element.54.qkv_ref, f32[1024,128]{1,0:T(8,128)S(1)} %copy.48.cos_ref, f32[1024,128]{1,0:T(8,128)S(1)} %copy.49.sin_ref, ...), custom_call_target="tpu_custom_call" | custom-call | tf_op jit(solution)/shard_map/attend_back/pallas_call | solution.py:169
  451.4 10.0 %convolution_convert_fusion.10 = bf16[512,2048]{1,0:T(8,128)(2,1)} fusion(bf16[2048,2176]{1,0:T(8,128)(2,1)} %constant_dynamic-update-slice_fusion.5, bf16[1024,2176]{1,0:T(8,128)(2,1)S(1)} %get-tuple-element.55), kind=kOutput, calls=%fused_computation.26 | convolution fusion | flops 4564451328 | bytes 13238272 | tf_op jit(solution)/shard_map/dot_general | solution.py:449
  461.5 6.3 convolution_convert_fusion.8.refs_0_
  471.5 120.3 %pick_rows.1 = (bf16[112,2048]{1,0:T(8,128)(2,1)}, bf16[128,2048]{1,0:T(8,128)(2,1)}, bf16[112,2048]{1,0:T(8,128)(2,1)}, bf16[128,2048]{1,0:T(8,128)(2,1)}, bf16...) custom-call(s32[1]{0:T(128)} %bitcast.10.index_ref, ...), custom_call_target="tpu_custom_call" | custom-call | tf_op jit(solution)/shard_map/pick_rows/pallas_call | solution.py:277
  606.8 6.3 collective-permute-done.52
  620.2 12.7 %collective-permute-done.57 = bf16[112,2048]{1,0:T(8,128)(2,1)} collective-permute-done((bf16[112,2048]{1,0:T(8,128)(2,1)}, bf16[112,2048]{1,0:T(8,128)(2,1)}, u32[]{:S(2)}, u32[]{:S(2)}) %collective-permute-start.57) | collective-permute-done | bytes 458784 | tf_op jit(solution)/shard_map/ppermute | solution.py:437
  638.7 35.2 %collective-permute-done.40 = bf16[256,2176]{1,0:T(8,128)(2,1)S(1)} collective-permute-done((bf16[256,2176]{1,0:T(8,128)(2,1)}, bf16[256,2176]{1,0:T(8,128)(2,1)S(1)}, u32[]{:S(2)}, u32[]{:S(2)}) %collective-permute-start.40) | collective-permute-done | bytes 1114144 | tf_op jit(solution)/shard_map/ppermute | solution.py:437
  682.1 10.7 %fusion.60 = (bf16[512,2048]{1,0:T(8,128)(2,1)S(1)}, f32[512,2048]{1,0:T(8,128)}) fusion(bf16[512,2048]{1,0:T(8,128)(2,1)} %copy-done.39, bf16[2048,2176]{1,0:T(8,128)(2,1)} %constant_dynamic-update-slice_fusion.5, bf16[1024,2176]{1,0:T(8,128)(2,1)S(1)} %bitcast.56), kind=kOutput, calls=%fused_computation.152 | convolution fusion | flops 4566548480 | bytes 19529728 | tf_op jit(solution)/shard_map/dot_general | solution.py:451
  694.0 7.8 collective-permute-start.36
  721.9 68.7 %cut_rows.1 = (bf16[64,2176]{1,0:T(8,128)(2,1)}, bf16[64,2176]{1,0:T(8,128)(2,1)}, bf16[64,2176]{1,0:T(8,128)(2,1)}, bf16[64,2176]{1,0:T(8,128)(2,1)}, bf16[64,2...) custom-call(s32[1]{0:T(128)} %bitcast.5.member_ref.index_ref, ...), custom_call_target="tpu_custom_call" | custom-call | tf_op jit(solution)/shard_map/cut_rows/pallas_call | solution.py:277
  815.6 17.1 %collective-permute-done.49.refs_5_ = bf16[64,2176]{1,0:T(8,128)(2,1)S(1)} collective-permute-done((bf16[64,2176]{1,0:T(8,128)(2,1)}, bf16[64,2176]{1,0:T(8,128)(2,1)S(1)}, u32[]{:S(2)}, u32[]{:S(2)}) %collective-permute-start.49) | collective-permute-done | bytes 278560 | tf_op jit(solution)/shard_map/ppermute | solution.py:437
  851.2 28.1 %collective-permute-start.62 = (f32[320]{0:T(512)S(1)}, f32[320]{0:T(512)S(1)}, u32[]{:S(2)}, u32[]{:S(2)}) collective-permute-start(f32[320]{0:T(512)S(1)} %get-tuple-element.80), channel_id=1, source_target_pairs={{0,8},{1,9},{2,10},{3,11},{4,12},{5,13},{6,14},{7,15},{8,0},{9,1},... | collective-permute-start | bytes 3848 | tf_op jit(solution)/shard_map/ppermute | solution.py:437
  881.1 9.2 %collective-permute-done.29 = bf16[128,2048]{1,0:T(8,128)(2,1)S(1)} collective-permute-done((bf16[128,2048]{1,0:T(8,128)(2,1)S(1)}, bf16[128,2048]{1,0:T(8,128)(2,1)S(1)}, u32[]{:S(2)}, u32[]{:S(2)}) %collective-permute-start.29) | collective-permute-done | bytes 524320 | tf_op jit(solution)/shard_map/ppermute | solution.py:437
  (323 shorter events, 218.3 us)
Async XLA Ops:
  43.0 48.4 %collective-permute-start.10 = (bf16[64,2176]{1,0:T(8,128)(2,1)S(1)}, bf16[64,2176]{1,0:T(8,128)(2,1)}, u32[]{:S(2)}, u32[]{:S(2)}) collective-permute-start(bf16[64,2176]{1,0:T(8,128)(2,1)S(1)} %get-tuple-element.50), channel_id=1, source_target_pairs={{0,25},{1,24},{2,27},{3,26},{4,29},{5,28},{6,31},{7,30},{8,17},{9,... | collective-permute-start | bytes 835592 | tf_op jit(solution)/shard_map/ppermute | solution.py:437
  46.3 141.4 %collective-permute-start.23 = (bf16[112,2048]{1,0:T(8,128)(2,1)}, bf16[112,2048]{1,0:T(8,128)(2,1)}, u32[]{:S(2)}, u32[]{:S(2)}) collective-permute-start(bf16[112,2048]{1,0:T(8,128)(2,1)} %slice.95.refs_0_), channel_id=1, source_target_pairs={{0,4},{1,5},{2,6},{3,7},{4,0},{5,1},{6,2},{7,3},{8,12},{9,13},{10,... | collective-permute-start | bytes 1376264 | tf_op jit(solution)/shard_map/ppermute | solution.py:437
  47.7 142.2 %collective-permute-start.21 = (bf16[112,2048]{1,0:T(8,128)(2,1)}, bf16[112,2048]{1,0:T(8,128)(2,1)}, u32[]{:S(2)}, u32[]{:S(2)}) collective-permute-start(bf16[112,2048]{1,0:T(8,128)(2,1)} %slice.95.refs_0_), channel_id=1, source_target_pairs={{0,2},{1,3},{2,0},{3,1},{4,6},{5,7},{6,4},{7,5},{8,10},{9,11},{10,... | collective-permute-start | bytes 1376264 | tf_op jit(solution)/shard_map/ppermute | solution.py:437
  70.0 109.9 %collective-permute-start.2 = (bf16[128,2048]{1,0:T(8,128)(2,1)}, bf16[128,2048]{1,0:T(8,128)(2,1)}, u32[]{:S(2)}, u32[]{:S(2)}) collective-permute-start(bf16[128,2048]{1,0:T(8,128)(2,1)} %copy-done.11), channel_id=1, source_target_pairs={{0,24},{1,25},{2,26},{3,27},{4,28},{5,29},{6,30},{7,31},{8,16},{9,... | collective-permute-start | bytes 1572872 | tf_op jit(solution)/shard_map/ppermute | solution.py:437
  73.7 107.6 %collective-permute-start.1 = (bf16[128,2048]{1,0:T(8,128)(2,1)}, bf16[128,2048]{1,0:T(8,128)(2,1)}, u32[]{:S(2)}, u32[]{:S(2)}) collective-permute-start(bf16[128,2048]{1,0:T(8,128)(2,1)} %copy-done.11), channel_id=1, source_target_pairs={{0,16},{1,17},{2,18},{3,19},{4,20},{5,21},{6,22},{7,23},{8,24},{9,... | collective-permute-start | bytes 1572872 | tf_op jit(solution)/shard_map/ppermute | solution.py:437
  91.3 91.5 %collective-permute-start = (bf16[128,2048]{1,0:T(8,128)(2,1)}, bf16[128,2048]{1,0:T(8,128)(2,1)}, u32[]{:S(2)}, u32[]{:S(2)}) collective-permute-start(bf16[128,2048]{1,0:T(8,128)(2,1)} %copy-done.11), channel_id=1, source_target_pairs={{0,8},{1,9},{2,10},{3,11},{4,12},{5,13},{6,14},{7,15},{8,0},{9,1},... | collective-permute-start | bytes 1572872 | tf_op jit(solution)/shard_map/ppermute | solution.py:437
  189.9 46.3 %collective-permute-start.32 = (bf16[128,2048]{1,0:T(8,128)(2,1)S(1)}, bf16[128,2048]{1,0:T(8,128)(2,1)S(1)}, u32[]{:S(2)}, u32[]{:S(2)}) collective-permute-start(bf16[128,2048]{1,0:T(8,128)(2,1)S(1)} %copy-done.16), channel_id=1, source_target_pairs={{0,16},{1,17},{2,18},{3,19},{4,20},{5,21},{6,22},{7,23},{8,24},{9,... | collective-permute-start | bytes 1572872 | tf_op jit(solution)/shard_map/ppermute | solution.py:437
  193.2 181.8 %collective-permute-start.11 = (bf16[256,2176]{1,0:T(8,128)(2,1)}, bf16[256,2176]{1,0:T(8,128)(2,1)}, u32[]{:S(2)}, u32[]{:S(2)}) collective-permute-start(bf16[256,2176]{1,0:T(8,128)(2,1)} %get-tuple-element.51), channel_id=1, source_target_pairs={{0,2},{1,3},{2,0},{3,1},{4,6},{5,7},{6,4},{7,5},{8,10},{9,11},{10,... | collective-permute-start | bytes 3342344 | tf_op jit(solution)/shard_map/ppermute | solution.py:437
  199.1 178.4 %collective-permute-start.14 = (bf16[256,2176]{1,0:T(8,128)(2,1)}, bf16[256,2176]{1,0:T(8,128)(2,1)}, u32[]{:S(2)}, u32[]{:S(2)}) collective-permute-start(bf16[256,2176]{1,0:T(8,128)(2,1)} %get-tuple-element.52), channel_id=1, source_target_pairs={{0,4},{1,5},{2,6},{3,7},{4,0},{5,1},{6,2},{7,3},{8,12},{9,13},{10,... | collective-permute-start | bytes 3342344 | tf_op jit(solution)/shard_map/ppermute | solution.py:437
  209.1 169.6 %collective-permute-start.12 = (bf16[256,2176]{1,0:T(8,128)(2,1)}, bf16[256,2176]{1,0:T(8,128)(2,1)}, u32[]{:S(2)}, u32[]{:S(2)}) collective-permute-start(bf16[256,2176]{1,0:T(8,128)(2,1)} %get-tuple-element.52), channel_id=1, source_target_pairs={{0,2},{1,3},{2,0},{3,1},{4,6},{5,7},{6,4},{7,5},{8,10},{9,11},{10,... | collective-permute-start | bytes 3342344 | tf_op jit(solution)/shard_map/ppermute | solution.py:437
  237.6 144.9 %collective-permute-start.13 = (bf16[256,2176]{1,0:T(8,128)(2,1)}, bf16[256,2176]{1,0:T(8,128)(2,1)}, u32[]{:S(2)}, u32[]{:S(2)}) collective-permute-start(bf16[256,2176]{1,0:T(8,128)(2,1)} %get-tuple-element.51), channel_id=1, source_target_pairs={{0,4},{1,5},{2,6},{3,7},{4,0},{5,1},{6,2},{7,3},{8,12},{9,13},{10,... | collective-permute-start | bytes 3342344 | tf_op jit(solution)/shard_map/ppermute | solution.py:437
  253.9 157.7 %collective-permute-start.3 = (bf16[512,2048]{1,0:T(8,128)(2,1)}, bf16[512,2048]{1,0:T(8,128)(2,1)}, u32[]{:S(2)}, u32[]{:S(2)}) collective-permute-start(bf16[512,2048]{1,0:T(8,128)(2,1)} %pad_maximum_fusion), channel_id=1, source_target_pairs={{0,1},{1,0},{2,3},{3,2},{4,5},{5,4},{6,7},{7,6},{8,9},{9,8},{10,11... | collective-permute-start | bytes 6291464 | tf_op jit(solution)/shard_map/ppermute | solution.py:437
  618.1 88.7 %collective-permute-start.39 = (bf16[256,2176]{1,0:T(8,128)(2,1)}, bf16[256,2176]{1,0:T(8,128)(2,1)S(1)}, u32[]{:S(2)}, u32[]{:S(2)}) collective-permute-start(bf16[256,2176]{1,0:T(8,128)(2,1)} %convolution_convert_fusion.6), channel_id=1, source_target_pairs={{0,2},{1,3},{2,0},{3,1},{4,6},{5,7},{6,4},{7,5},{8,10},{9,11},{10,... | collective-permute-start | bytes 3342344 | tf_op jit(solution)/shard_map/ppermute | solution.py:437
  619.2 54.8 %collective-permute-start.40 = (bf16[256,2176]{1,0:T(8,128)(2,1)}, bf16[256,2176]{1,0:T(8,128)(2,1)S(1)}, u32[]{:S(2)}, u32[]{:S(2)}) collective-permute-start(bf16[256,2176]{1,0:T(8,128)(2,1)} %convolution_convert_fusion.4), channel_id=1, source_target_pairs={{0,2},{1,3},{2,0},{3,1},{4,6},{5,7},{6,4},{7,5},{8,10},{9,11},{10,... | collective-permute-start | bytes 3342344 | tf_op jit(solution)/shard_map/ppermute | solution.py:437
  632.9 43.5 %collective-permute-start.42 = (bf16[256,2176]{1,0:T(8,128)(2,1)}, bf16[256,2176]{1,0:T(8,128)(2,1)S(1)}, u32[]{:S(2)}, u32[]{:S(2)}) collective-permute-start(bf16[256,2176]{1,0:T(8,128)(2,1)} %convolution_convert_fusion.1), channel_id=1, source_target_pairs={{0,4},{1,5},{2,6},{3,7},{4,0},{5,1},{6,2},{7,3},{8,12},{9,13},{10,... | collective-permute-start | bytes 3342344 | tf_op jit(solution)/shard_map/ppermute | solution.py:437
  635.5 82.8 %collective-permute-start.44 = (bf16[256,2176]{1,0:T(8,128)(2,1)}, bf16[256,2176]{1,0:T(8,128)(2,1)S(1)}, u32[]{:S(2)}, u32[]{:S(2)}) collective-permute-start(bf16[256,2176]{1,0:T(8,128)(2,1)} %convolution_convert_fusion), channel_id=1, source_target_pairs={{0,4},{1,5},{2,6},{3,7},{4,0},{5,1},{6,2},{7,3},{8,12},{9,13},{10,... | collective-permute-start | bytes 3342344 | tf_op jit(solution)/shard_map/ppermute | solution.py:437
  636.4 43.4 %collective-permute-start.35 = (bf16[512,2048]{1,0:T(8,128)(2,1)}, bf16[512,2048]{1,0:T(8,128)(2,1)S(1)}, u32[]{:S(2)}, u32[]{:S(2)}) collective-permute-start(bf16[512,2048]{1,0:T(8,128)(2,1)} %convolution_convert_fusion.10), channel_id=1, source_target_pairs={{0,1},{1,0},{2,3},{3,2},{4,5},{5,4},{6,7},{7,6},{8,9},{9,8},{10,11... | collective-permute-start | bytes 6291464 | tf_op jit(solution)/shard_map/ppermute | solution.py:437
  694.0 96.6 %collective-permute-start.36 = (bf16[128,2048]{1,0:T(8,128)(2,1)}, bf16[128,2048]{1,0:T(8,128)(2,1)S(1)}, u32[]{:S(2)}, u32[]{:S(2)}) collective-permute-start(bf16[128,2048]{1,0:T(8,128)(2,1)} %get-tuple-element.86), channel_id=1, source_target_pairs={{0,8},{1,9},{2,10},{3,11},{4,12},{5,13},{6,14},{7,15},{8,0},{9,1},... | collective-permute-start | bytes 1572872 | tf_op jit(solution)/shard_map/ppermute | solution.py:437
  706.8 85.6 %collective-permute-start.38 = (bf16[128,2048]{1,0:T(8,128)(2,1)}, bf16[128,2048]{1,0:T(8,128)(2,1)S(1)}, u32[]{:S(2)}, u32[]{:S(2)}) collective-permute-start(bf16[128,2048]{1,0:T(8,128)(2,1)} %get-tuple-element.87), channel_id=1, source_target_pairs={{0,24},{1,25},{2,26},{3,27},{4,28},{5,29},{6,30},{7,31},{8,16},{9,... | collective-permute-start | bytes 1572872 | tf_op jit(solution)/shard_map/ppermute | solution.py:437
  710.0 83.3 %collective-permute-start.37 = (bf16[128,2048]{1,0:T(8,128)(2,1)}, bf16[128,2048]{1,0:T(8,128)(2,1)S(1)}, u32[]{:S(2)}, u32[]{:S(2)}) collective-permute-start(bf16[128,2048]{1,0:T(8,128)(2,1)} %get-tuple-element.88), channel_id=1, source_target_pairs={{0,16},{1,17},{2,18},{3,19},{4,20},{5,21},{6,22},{7,23},{8,24},{9,... | collective-permute-start | bytes 1572872 | tf_op jit(solution)/shard_map/ppermute | solution.py:437
  815.6 65.5 %collective-permute-start.28 = (bf16[128,2048]{1,0:T(8,128)(2,1)S(1)}, bf16[128,2048]{1,0:T(8,128)(2,1)S(1)}, u32[]{:S(2)}, u32[]{:S(2)}) collective-permute-start(bf16[128,2048]{1,0:T(8,128)(2,1)S(1)} %get-tuple-element.89), channel_id=1, source_target_pairs={{0,8},{1,9},{2,10},{3,11},{4,12},{5,13},{6,14},{7,15},{8,0},{9,1},... | collective-permute-start | bytes 1572872 | tf_op jit(solution)/shard_map/ppermute | solution.py:437
  832.7 48.4 %collective-permute-start.30 = (bf16[128,2048]{1,0:T(8,128)(2,1)S(1)}, bf16[128,2048]{1,0:T(8,128)(2,1)S(1)}, u32[]{:S(2)}, u32[]{:S(2)}) collective-permute-start(bf16[128,2048]{1,0:T(8,128)(2,1)S(1)} %get-tuple-element.90), channel_id=1, source_target_pairs={{0,24},{1,25},{2,26},{3,27},{4,28},{5,29},{6,30},{7,31},{8,16},{9,... | collective-permute-start | bytes 1572872 | tf_op jit(solution)/shard_map/ppermute | solution.py:437
  833.4 56.8 %collective-permute-start.29 = (bf16[128,2048]{1,0:T(8,128)(2,1)S(1)}, bf16[128,2048]{1,0:T(8,128)(2,1)S(1)}, u32[]{:S(2)}, u32[]{:S(2)}) collective-permute-start(bf16[128,2048]{1,0:T(8,128)(2,1)S(1)} %get-tuple-element.91), channel_id=1, source_target_pairs={{0,16},{1,17},{2,18},{3,19},{4,20},{5,21},{6,22},{7,23},{8,24},{9,... | collective-permute-start | bytes 1572872 | tf_op jit(solution)/shard_map/ppermute | solution.py:437
  851.2 41.9 %collective-permute-start.62 = (f32[320]{0:T(512)S(1)}, f32[320]{0:T(512)S(1)}, u32[]{:S(2)}, u32[]{:S(2)}) collective-permute-start(f32[320]{0:T(512)S(1)} %get-tuple-element.80), channel_id=1, source_target_pairs={{0,8},{1,9},{2,10},{3,11},{4,12},{5,13},{6,14},{7,15},{8,0},{9,1},... | collective-permute-start | bytes 3848 | tf_op jit(solution)/shard_map/ppermute | solution.py:437
  (84 other events, 2031.3 us)

commit v3 on v2

--- a/solution.py
+++ b/solution.py
@@ -267,19 +267,21 @@
             pl.when(when)(copy.wait)
 
 
-def mover(pairs_of, index, arrays, shapes, copies, name):
+def mover(pairs_of, index, arrays, shapes, copies, name, inward):
     count = len(arrays)
 
     def kernel(index_ref, *refs):
         move_all(pairs_of, index_ref[0], refs[:count], refs[count:-1], refs[-1])
 
     anywhere = pl.BlockSpec(memory_space=pl.ANY)
+    held = pl.BlockSpec(memory_space=pltpu.VMEM)
     return pl.pallas_call(
         kernel,
-        in_specs=[pl.BlockSpec(memory_space=pltpu.SMEM)] + [anywhere] * count,
-        out_specs=[anywhere] * len(shapes),
+        in_specs=[pl.BlockSpec(memory_space=pltpu.SMEM)] + [anywhere if inward else held] * count,
+        out_specs=[held if inward else anywhere] * len(shapes),
         out_shape=[jax.ShapeDtypeStruct(shape, BF) for shape in shapes],
         scratch_shapes=[pltpu.SemaphoreType.DMA((copies,))],
+        compiler_params=pltpu.CompilerParams(vmem_limit_bytes=16 << 20),
         name=name,
     )(index, *arrays)
 
@@ -299,7 +301,7 @@
                 out.append((spot // half == h, ins[r], dst, sem.at[r]))
         return out
 
-    return mover(pairs, member, parts, [(half * rows, width)] * 2, tp, "stack_rows")
+    return mover(pairs, member, parts, [(half * rows, width)] * 2, tp, "stack_rows", True)
 
 
 def cut_call(member, low, high, tp):
@@ -317,7 +319,7 @@
                 out.append((spot // half == h, src, outs[r], sem.at[r]))
         return out
 
-    return mover(pairs, member, [low, high], [(rows, width)] * tp, tp, "cut_rows")
+    return mover(pairs, member, [low, high], [(rows, width)] * tp, tp, "cut_rows", False)
 
 
 def row_pairs(me, wide, own, own_ff, cut, halves, whole, sem, inward):
@@ -347,7 +349,7 @@
         return row_pairs(me, wide, own, own_ff, cut, ins, outs[0], sem, True)
 
     shape = (wide * (own + own_ff), width)
-    return mover(pairs, lane, arrays, [shape], 3 * wide, "place_rows")[0]
+    return mover(pairs, lane, arrays, [shape], 3 * wide, "place_rows", True)[0]
 
 
 def pick_call(lane, part, wide, own, own_ff, cut):
@@ -357,7 +359,7 @@
         return row_pairs(me, wide, own, own_ff, cut, outs, ins[0], sem, False)
 
     shapes = [(cut, width), (own + own_ff - cut, width)] * wide
-    outs = mover(pairs, lane, [part], shapes, 3 * wide, "pick_rows")
+    outs = mover(pairs, lane, [part], shapes, 3 * wide, "pick_rows", False)
     return [outs[2 * j : 2 * j + 2] for j in range(wide)]
 
 

time: 905 us -> 557 us (0.62)
  Pallas kernels: 401 us -> 29.7 us
  waiting for transfers between devices: 179 us -> 210 us
  starting transfers between devices: 145 us -> 173 us
  local copies, waits for them, and re-layouts: 54.6 us -> 34.9 us
    pallas_call x4, Pallas kernels: 378 us -> 5.68 us  [mover(): pl.pallas_call(kernel, in_specs=[pl.BlockSpec(memory_space=pltpu.SMEM)] +...]
    ppermute x65, waiting for transfers between devices: 179 us -> 210 us  [send(): return lax.ppermute(value, AXES, pairs)]
    ppermute x65, starting transfers between devices: 145 us -> 173 us  [send(): return lax.ppermute(value, AXES, pairs)]
    unnamed x104 -> x70, local copies, waits for them, and re-layouts: 31.6 us -> 14.2 us
  transfers between devices with their start and end apart: 65 -> 65, of which waited for: 18 -> 21; matrix products, arithmetic and copies ran while one was open for 13% -> 17% of each run, Pallas kernels for 29% -> 2%
where the time goes in v3:
time: 557 us; the launch traced here: 550 us
  waiting for transfers between devices  210 us (38%)
  starting transfers between devices  173 us (31%)
  matrix products  74.7 us (13%)
  local copies, waits for them, and re-layouts  34.9 us (6%)
  Pallas kernels  29.7 us (5%)
  other arithmetic  26.2 us (5%)
    ppermute x65, waiting for transfers between devices, send(): return lax.ppermute(value, AXES, pairs)  210 us
    ppermute x65, starting transfers between devices, send(): return lax.ppermute(value, AXES, pairs)  173 us
    dot_general x8, matrix products, columns_out(): lax.dot_general(lhs[:, at:at + size], rhs, CONTRACT_ROWS, preferred_eleme...  20.1 us
    dot_general x2, matrix products, scatter_tokens(): near = lax.dot_general(lhs[:half], rhs, dims, preferred_element_type=F32)  17.1 us
    dot_general x1, matrix products, on_device(): proj = jnp.dot(normed_all, entry, preferred_element_type=F32)  14.6 us
    unnamed x70, local copies, waits for them, and re-layouts  14.2 us
    dot_general x2, matrix products, scatter_tokens(): lax.dot_general(lhs[half:], rhs, dims, preferred_element_type=F32)  13.7 us
  transfers between devices with their start and end apart: 65, of which 21 were waited for; matrix products, arithmetic and copies ran while one was open for 17% of the time, Pallas kernels for 2%

profile of v3, /device:TPU:0, one launch (start us, length us, event | category | flops | bytes accessed | tf_op | source)
XLA Modules:
  0.0 550.1 jit_solution(3806437778960329690)
XLA Ops:
  44.4 21.0 %collective-permute-done.8.refs_5_ = bf16[64,2176]{1,0:T(8,128)(2,1)} collective-permute-done((bf16[64,2176]{1,0:T(8,128)(2,1)}, bf16[64,2176]{1,0:T(8,128)(2,1)}, u32[]{:S(2)}, u32[]{:S(2)}) %collective-permute-start.8) | collective-permute-done | bytes 278560 | tf_op jit(solution)/shard_map/ppermute | solution.py:439
  69.2 17.4 %collective-permute-start.1 = (bf16[128,2048]{1,0:T(8,128)(2,1)}, bf16[128,2048]{1,0:T(8,128)(2,1)S(1)}, u32[]{:S(2)}, u32[]{:S(2)}) collective-permute-start(bf16[128,2048]{1,0:T(8,128)(2,1)} %copy-done.9), channel_id=1, source_target_pairs={{0,16},{1,17},{2,18},{3,19},{4,20},{5,21},{6,22},{7,23},{8,24},{9,... | collective-permute-start | bytes 1572872 | tf_op jit(solution)/shard_map/ppermute | solution.py:439
  86.6 15.3 %collective-permute-start = (bf16[128,2048]{1,0:T(8,128)(2,1)}, bf16[128,2048]{1,0:T(8,128)(2,1)S(1)}, u32[]{:S(2)}, u32[]{:S(2)}) collective-permute-start(bf16[128,2048]{1,0:T(8,128)(2,1)} %copy-done.9), channel_id=1, source_target_pairs={{0,8},{1,9},{2,10},{3,11},{4,12},{5,13},{6,14},{7,15},{8,0},{9,1},... | collective-permute-start | bytes 1572872 | tf_op jit(solution)/shard_map/ppermute | solution.py:439
  107.1 15.8 %collective-permute-done.1 = bf16[128,2048]{1,0:T(8,128)(2,1)S(1)} collective-permute-done((bf16[128,2048]{1,0:T(8,128)(2,1)}, bf16[128,2048]{1,0:T(8,128)(2,1)S(1)}, u32[]{:S(2)}, u32[]{:S(2)}) %collective-permute-start.1) | collective-permute-done | bytes 524320 | tf_op jit(solution)/shard_map/ppermute | solution.py:439
  130.7 7.1 %collective-permute-done.31 = bf16[128,2048]{1,0:T(8,128)(2,1)S(1)} collective-permute-done((bf16[128,2048]{1,0:T(8,128)(2,1)S(1)}, bf16[128,2048]{1,0:T(8,128)(2,1)S(1)}, u32[]{:S(2)}, u32[]{:S(2)}) %collective-permute-start.31) | collective-permute-done | bytes 524320 | tf_op jit(solution)/shard_map/ppermute | solution.py:439
  139.9 12.3 %collective-permute-done.33 = bf16[128,2048]{1,0:T(8,128)(2,1)S(1)} collective-permute-done((bf16[128,2048]{1,0:T(8,128)(2,1)S(1)}, bf16[128,2048]{1,0:T(8,128)(2,1)S(1)}, u32[]{:S(2)}, u32[]{:S(2)}) %collective-permute-start.33) | collective-permute-done | bytes 524320 | tf_op jit(solution)/shard_map/ppermute | solution.py:439
  153.7 20.9 %collective-permute-done.32 = bf16[128,2048]{1,0:T(8,128)(2,1)S(1)} collective-permute-done((bf16[128,2048]{1,0:T(8,128)(2,1)S(1)}, bf16[128,2048]{1,0:T(8,128)(2,1)S(1)}, u32[]{:S(2)}, u32[]{:S(2)}) %collective-permute-start.32) | collective-permute-done | bytes 524320 | tf_op jit(solution)/shard_map/ppermute | solution.py:439
  178.0 17.2 %collective-permute-done.26.refs_7_ = bf16[128,2048]{1,0:T(8,128)(2,1)S(1)} collective-permute-done((bf16[128,2048]{1,0:T(8,128)(2,1)S(1)}, bf16[128,2048]{1,0:T(8,128)(2,1)S(1)}, u32[]{:S(2)}, u32[]{:S(2)}) %collective-permute-start.26) | collective-permute-done | bytes 524320 | tf_op jit(solution)/shard_map/ppermute | solution.py:439
  205.7 19.9 %collective-permute-done.15 = bf16[256,2176]{1,0:T(8,128)(2,1)S(1)} collective-permute-done((bf16[256,2176]{1,0:T(8,128)(2,1)S(1)}, bf16[256,2176]{1,0:T(8,128)(2,1)S(1)}, u32[]{:S(2)}, u32[]{:S(2)}) %collective-permute-start.15) | collective-permute-done | bytes 1114144 | tf_op jit(solution)/shard_map/ppermute | solution.py:439
  232.9 14.6 %fusion.62.proj_ref = f32[1024,2176]{1,0:T(8,128)S(1)} fusion(bf16[1024,2048]{1,0:T(8,128)(2,1)S(1)} %constant_dynamic-update-slice_fusion, bf16[2048,2176]{1,0:T(8,128)(2,1)} %constant_dynamic-update-slice_fusion.5), kind=kOutput, calls=%fused_computation.154 | convolution fusion | flops 9126805504 | bytes 22020096 | tf_op jit(solution)/shard_map/dot_general | solution.py:591
  247.5 7.3 %attend.1 = (bf16[1024,960]{1,0:T(8,128)(2,1)S(1)}, bf16[1024,768]{1,0:T(8,128)(2,1)S(1)}) custom-call(f32[1024,2176]{1,0:T(8,128)S(1)} %fusion.62.proj_ref, f32[8,768]{1,0:T(8,128)S(1)} %broadcast_in_dim.36.bqkv_ref, f32[1024,128]{1,0:T(8,128)S(1)} %copy.48.cos_ref, f32[1024,128]{1,0:T(8,128)S(1)} %copy.49.sin_ref, f32[8,128,128]{2,1,0:T(8,128)S(1)} %and_select_fusion.mask_ref), custom_call_target="tpu_custom_call" | custom-call | tf_op jit(solution)/shard_map/attend/pallas_call | solution.py:155
  254.8 11.0 %attend_back.1 = (bf16[1024,2176]{1,0:T(8,128)(2,1)S(1)}, f32[8,768]{1,0:T(8,128)S(1)}) custom-call(f32[1024,2176]{1,0:T(8,128)S(1)} %fusion.62.proj_ref, f32[1024,960]{1,0:T(8,128)S(1)} %fusion.63.back_ref, bf16[1024,768]{1,0:T(8,128)(2,1)S(1)} %get-tuple-element.54.qkv_ref, f32[1024,128]{1,0:T(8,128)S(1)} %copy.48.cos_ref, f32[1024,128]{1,0:T(8,128)S(1)} %copy.49.sin_ref, ...), custom_call_target="tpu_custom_call" | custom-call | tf_op jit(solution)/shard_map/attend_back/pallas_call | solution.py:169
  269.7 10.1 %convolution_convert_fusion.10 = bf16[512,2048]{1,0:T(8,128)(2,1)} fusion(bf16[2048,2176]{1,0:T(8,128)(2,1)} %constant_dynamic-update-slice_fusion.5, bf16[1024,2176]{1,0:T(8,128)(2,1)S(1)} %get-tuple-element.55), kind=kOutput, calls=%fused_computation.26 | convolution fusion | flops 4564451328 | bytes 13238272 | tf_op jit(solution)/shard_map/dot_general | solution.py:451
  304.3 5.1 collective-permute-done.52
  317.0 11.0 %collective-permute-done.57 = bf16[112,2048]{1,0:T(8,128)(2,1)} collective-permute-done((bf16[112,2048]{1,0:T(8,128)(2,1)}, bf16[112,2048]{1,0:T(8,128)(2,1)}, u32[]{:S(2)}, u32[]{:S(2)}) %collective-permute-start.57) | collective-permute-done | bytes 458784 | tf_op jit(solution)/shard_map/ppermute | solution.py:439
  335.2 34.5 %collective-permute-done.40 = bf16[256,2176]{1,0:T(8,128)(2,1)S(1)} collective-permute-done((bf16[256,2176]{1,0:T(8,128)(2,1)}, bf16[256,2176]{1,0:T(8,128)(2,1)S(1)}, u32[]{:S(2)}, u32[]{:S(2)}) %collective-permute-start.40) | collective-permute-done | bytes 1114144 | tf_op jit(solution)/shard_map/ppermute | solution.py:439
  376.8 10.6 %fusion.60 = (bf16[512,2048]{1,0:T(8,128)(2,1)S(1)}, f32[512,2048]{1,0:T(8,128)}) fusion(bf16[512,2048]{1,0:T(8,128)(2,1)} %copy-done.23, bf16[2048,2176]{1,0:T(8,128)(2,1)} %constant_dynamic-update-slice_fusion.5, bf16[1024,2176]{1,0:T(8,128)(2,1)S(1)} %bitcast.56), kind=kOutput, calls=%fused_computation.152 | convolution fusion | flops 4566548480 | bytes 19529728 | tf_op jit(solution)/shard_map/dot_general | solution.py:453
  392.0 6.6 %fusion.61 = (bf16[512,2048]{1,0:T(8,128)(2,1)}, f32[512,2048]{1,0:T(8,128)}) fusion(bf16[512,2048]{1,0:T(8,128)(2,1)} %collective-permute-done.27, bf16[960,2048]{1,0:T(8,128)(2,1)S(1)} %copy-done.2, bf16[1024,960]{1,0:T(8,128)(2,1)S(1)} %get-tuple-element.53), kind=kOutput, calls=%fused_computation.153 | convolution fusion | flops 2016411648 | bytes 13369344 | tf_op jit(solution)/shard_map/dot_general | solution.py:453
  413.8 7.4 %collective-permute-done.38 = bf16[128,2048]{1,0:T(8,128)(2,1)S(1)} collective-permute-done((bf16[128,2048]{1,0:T(8,128)(2,1)S(1)}, bf16[128,2048]{1,0:T(8,128)(2,1)S(1)}, u32[]{:S(2)}, u32[]{:S(2)}) %collective-permute-start.38) | collective-permute-done | bytes 524320 | tf_op jit(solution)/shard_map/ppermute | solution.py:439
  421.2 19.8 %collective-permute-start.48 = (bf16[64,2176]{1,0:T(8,128)(2,1)S(1)}, bf16[64,2176]{1,0:T(8,128)(2,1)S(1)}, u32[]{:S(2)}, u32[]{:S(2)}) collective-permute-start(bf16[64,2176]{1,0:T(8,128)(2,1)S(1)} %get-tuple-element.60), channel_id=1, source_target_pairs={{0,16},{1,17},{2,18},{3,19},{4,20},{5,21},{6,22},{7,23},{8,24},{9,... | collective-permute-start | bytes 835592 | tf_op jit(solution)/shard_map/ppermute | solution.py:439
  440.9 15.7 %collective-permute-done.37 = bf16[128,2048]{1,0:T(8,128)(2,1)S(1)} collective-permute-done((bf16[128,2048]{1,0:T(8,128)(2,1)S(1)}, bf16[128,2048]{1,0:T(8,128)(2,1)S(1)}, u32[]{:S(2)}, u32[]{:S(2)}) %collective-permute-start.37) | collective-permute-done | bytes 524320 | tf_op jit(solution)/shard_map/ppermute | solution.py:439
  484.4 9.8 %collective-permute-start.29 = (bf16[128,2048]{1,0:T(8,128)(2,1)S(1)}, bf16[128,2048]{1,0:T(8,128)(2,1)S(1)}, u32[]{:S(2)}, u32[]{:S(2)}) collective-permute-start(bf16[128,2048]{1,0:T(8,128)(2,1)S(1)} %get-tuple-element.91), channel_id=1, source_target_pairs={{0,16},{1,17},{2,18},{3,19},{4,20},{5,21},{6,22},{7,23},{8,24},{9,... | collective-permute-start | bytes 1572872 | tf_op jit(solution)/shard_map/ppermute | solution.py:439
  505.9 29.7 %collective-permute-start.62 = (f32[320]{0:T(512)S(1)}, f32[320]{0:T(512)S(1)}, u32[]{:S(2)}, u32[]{:S(2)}) collective-permute-start(f32[320]{0:T(512)S(1)} %get-tuple-element.80), channel_id=1, source_target_pairs={{0,8},{1,9},{2,10},{3,11},{4,12},{5,13},{6,14},{7,15},{8,0},{9,1},... | collective-permute-start | bytes 3848 | tf_op jit(solution)/shard_map/ppermute | solution.py:439
  538.0 7.6 %collective-permute-done.29 = bf16[128,2048]{1,0:T(8,128)(2,1)S(1)} collective-permute-done((bf16[128,2048]{1,0:T(8,128)(2,1)S(1)}, bf16[128,2048]{1,0:T(8,128)(2,1)S(1)}, u32[]{:S(2)}, u32[]{:S(2)}) %collective-permute-start.29) | collective-permute-done | bytes 524320 | tf_op jit(solution)/shard_map/ppermute | solution.py:439
  (289 shorter events, 200.6 us)
Async XLA Ops:
  35.4 51.3 %collective-permute-start.10 = (bf16[64,2176]{1,0:T(8,128)(2,1)}, bf16[64,2176]{1,0:T(8,128)(2,1)}, u32[]{:S(2)}, u32[]{:S(2)}) collective-permute-start(bf16[64,2176]{1,0:T(8,128)(2,1)} %get-tuple-element.50), channel_id=1, source_target_pairs={{0,25},{1,24},{2,27},{3,26},{4,29},{5,28},{6,31},{7,30},{8,17},{9,... | collective-permute-start | bytes 835592 | tf_op jit(solution)/shard_map/ppermute | solution.py:439
  41.5 84.0 %collective-permute-start.23 = (bf16[112,2048]{1,0:T(8,128)(2,1)S(1)}, bf16[112,2048]{1,0:T(8,128)(2,1)S(1)}, u32[]{:S(2)}, u32[]{:S(2)}) collective-permute-start(bf16[112,2048]{1,0:T(8,128)(2,1)S(1)} %slice.95.refs_0_), channel_id=1, source_target_pairs={{0,4},{1,5},{2,6},{3,7},{4,0},{5,1},{6,2},{7,3},{8,12},{9,13},{10,... | collective-permute-start | bytes 1376264 | tf_op jit(solution)/shard_map/ppermute | solution.py:439
  42.9 85.5 %collective-permute-start.21 = (bf16[112,2048]{1,0:T(8,128)(2,1)S(1)}, bf16[112,2048]{1,0:T(8,128)(2,1)S(1)}, u32[]{:S(2)}, u32[]{:S(2)}) collective-permute-start(bf16[112,2048]{1,0:T(8,128)(2,1)S(1)} %slice.95.refs_0_), channel_id=1, source_target_pairs={{0,2},{1,3},{2,0},{3,1},{4,6},{5,7},{6,4},{7,5},{8,10},{9,11},{10,... | collective-permute-start | bytes 1376264 | tf_op jit(solution)/shard_map/ppermute | solution.py:439
  65.4 40.2 %collective-permute-start.2 = (bf16[128,2048]{1,0:T(8,128)(2,1)}, bf16[128,2048]{1,0:T(8,128)(2,1)S(1)}, u32[]{:S(2)}, u32[]{:S(2)}) collective-permute-start(bf16[128,2048]{1,0:T(8,128)(2,1)} %copy-done.9), channel_id=1, source_target_pairs={{0,24},{1,25},{2,26},{3,27},{4,28},{5,29},{6,30},{7,31},{8,16},{9,... | collective-permute-start | bytes 1572872 | tf_op jit(solution)/shard_map/ppermute | solution.py:439
  69.2 53.7 %collective-permute-start.1 = (bf16[128,2048]{1,0:T(8,128)(2,1)}, bf16[128,2048]{1,0:T(8,128)(2,1)S(1)}, u32[]{:S(2)}, u32[]{:S(2)}) collective-permute-start(bf16[128,2048]{1,0:T(8,128)(2,1)} %copy-done.9), channel_id=1, source_target_pairs={{0,16},{1,17},{2,18},{3,19},{4,20},{5,21},{6,22},{7,23},{8,24},{9,... | collective-permute-start | bytes 1572872 | tf_op jit(solution)/shard_map/ppermute | solution.py:439
  128.4 46.2 %collective-permute-start.32 = (bf16[128,2048]{1,0:T(8,128)(2,1)S(1)}, bf16[128,2048]{1,0:T(8,128)(2,1)S(1)}, u32[]{:S(2)}, u32[]{:S(2)}) collective-permute-start(bf16[128,2048]{1,0:T(8,128)(2,1)S(1)} %copy-done.15), channel_id=1, source_target_pairs={{0,16},{1,17},{2,18},{3,19},{4,20},{5,21},{6,22},{7,23},{8,24},{9,... | collective-permute-start | bytes 1572872 | tf_op jit(solution)/shard_map/ppermute | solution.py:439
  129.1 67.9 %collective-permute-start.11 = (bf16[256,2176]{1,0:T(8,128)(2,1)S(1)}, bf16[256,2176]{1,0:T(8,128)(2,1)S(1)}, u32[]{:S(2)}, u32[]{:S(2)}) collective-permute-start(bf16[256,2176]{1,0:T(8,128)(2,1)S(1)} %get-tuple-element.51), channel_id=1, source_target_pairs={{0,2},{1,3},{2,0},{3,1},{4,6},{5,7},{6,4},{7,5},{8,10},{9,11},{10,... | collective-permute-start | bytes 3342344 | tf_op jit(solution)/shard_map/ppermute | solution.py:439
  137.7 38.4 %collective-permute-start.25 = (bf16[112,2048]{1,0:T(8,128)(2,1)S(1)}, bf16[112,2048]{1,0:T(8,128)(2,1)S(1)}, u32[]{:S(2)}, u32[]{:S(2)}) collective-permute-start(bf16[112,2048]{1,0:T(8,128)(2,1)S(1)} %collective-permute-done.21.refs_2_), channel_id=1, source_target_pairs={{0,4},{1,5},{2,6},{3,7},{4,0},{5,1},{6,2},{7,3},{8,12},{9,13},{10,... | collective-permute-start | bytes 1376264 | tf_op jit(solution)/shard_map/ppermute | solution.py:439
  139.5 59.8 %collective-permute-start.14 = (bf16[256,2176]{1,0:T(8,128)(2,1)S(1)}, bf16[256,2176]{1,0:T(8,128)(2,1)S(1)}, u32[]{:S(2)}, u32[]{:S(2)}) collective-permute-start(bf16[256,2176]{1,0:T(8,128)(2,1)S(1)} %get-tuple-element.52), channel_id=1, source_target_pairs={{0,4},{1,5},{2,6},{3,7},{4,0},{5,1},{6,2},{7,3},{8,12},{9,13},{10,... | collective-permute-start | bytes 3342344 | tf_op jit(solution)/shard_map/ppermute | solution.py:439
  152.2 48.8 %collective-permute-start.12 = (bf16[256,2176]{1,0:T(8,128)(2,1)S(1)}, bf16[256,2176]{1,0:T(8,128)(2,1)S(1)}, u32[]{:S(2)}, u32[]{:S(2)}) collective-permute-start(bf16[256,2176]{1,0:T(8,128)(2,1)S(1)} %get-tuple-element.52), channel_id=1, source_target_pairs={{0,2},{1,3},{2,0},{3,1},{4,6},{5,7},{6,4},{7,5},{8,10},{9,11},{10,... | collective-permute-start | bytes 3342344 | tf_op jit(solution)/shard_map/ppermute | solution.py:439
  314.9 83.7 %collective-permute-start.39 = (bf16[256,2176]{1,0:T(8,128)(2,1)}, bf16[256,2176]{1,0:T(8,128)(2,1)S(1)}, u32[]{:S(2)}, u32[]{:S(2)}) collective-permute-start(bf16[256,2176]{1,0:T(8,128)(2,1)} %convolution_convert_fusion.6), channel_id=1, source_target_pairs={{0,2},{1,3},{2,0},{3,1},{4,6},{5,7},{6,4},{7,5},{8,10},{9,11},{10,... | collective-permute-start | bytes 3342344 | tf_op jit(solution)/shard_map/ppermute | solution.py:439
  316.4 53.2 %collective-permute-start.40 = (bf16[256,2176]{1,0:T(8,128)(2,1)}, bf16[256,2176]{1,0:T(8,128)(2,1)S(1)}, u32[]{:S(2)}, u32[]{:S(2)}) collective-permute-start(bf16[256,2176]{1,0:T(8,128)(2,1)} %convolution_convert_fusion.4), channel_id=1, source_target_pairs={{0,2},{1,3},{2,0},{3,1},{4,6},{5,7},{6,4},{7,5},{8,10},{9,11},{10,... | collective-permute-start | bytes 3342344 | tf_op jit(solution)/shard_map/ppermute | solution.py:439
  327.9 43.2 %collective-permute-start.42 = (bf16[256,2176]{1,0:T(8,128)(2,1)}, bf16[256,2176]{1,0:T(8,128)(2,1)S(1)}, u32[]{:S(2)}, u32[]{:S(2)}) collective-permute-start(bf16[256,2176]{1,0:T(8,128)(2,1)} %convolution_convert_fusion.1), channel_id=1, source_target_pairs={{0,4},{1,5},{2,6},{3,7},{4,0},{5,1},{6,2},{7,3},{8,12},{9,13},{10,... | collective-permute-start | bytes 3342344 | tf_op jit(solution)/shard_map/ppermute | solution.py:439
  330.9 78.1 %collective-permute-start.44 = (bf16[256,2176]{1,0:T(8,128)(2,1)}, bf16[256,2176]{1,0:T(8,128)(2,1)S(1)}, u32[]{:S(2)}, u32[]{:S(2)}) collective-permute-start(bf16[256,2176]{1,0:T(8,128)(2,1)} %convolution_convert_fusion), channel_id=1, source_target_pairs={{0,4},{1,5},{2,6},{3,7},{4,0},{5,1},{6,2},{7,3},{8,12},{9,13},{10,... | collective-permute-start | bytes 3342344 | tf_op jit(solution)/shard_map/ppermute | solution.py:439
  331.5 42.5 %collective-permute-start.35 = (bf16[512,2048]{1,0:T(8,128)(2,1)}, bf16[512,2048]{1,0:T(8,128)(2,1)S(1)}, u32[]{:S(2)}, u32[]{:S(2)}) collective-permute-start(bf16[512,2048]{1,0:T(8,128)(2,1)} %convolution_convert_fusion.10), channel_id=1, source_target_pairs={{0,1},{1,0},{2,3},{3,2},{4,5},{5,4},{6,7},{7,6},{8,9},{9,8},{10,11... | collective-permute-start | bytes 6291464 | tf_op jit(solution)/shard_map/ppermute | solution.py:439
  403.7 53.0 %collective-permute-start.37 = (bf16[128,2048]{1,0:T(8,128)(2,1)S(1)}, bf16[128,2048]{1,0:T(8,128)(2,1)S(1)}, u32[]{:S(2)}, u32[]{:S(2)}) collective-permute-start(bf16[128,2048]{1,0:T(8,128)(2,1)S(1)} %get-tuple-element.88), channel_id=1, source_target_pairs={{0,16},{1,17},{2,18},{3,19},{4,20},{5,21},{6,22},{7,23},{8,24},{9,... | collective-permute-start | bytes 1572872 | tf_op jit(solution)/shard_map/ppermute | solution.py:439
  411.5 61.2 %collective-permute-start.45 = (bf16[64,2176]{1,0:T(8,128)(2,1)}, bf16[64,2176]{1,0:T(8,128)(2,1)S(1)}, u32[]{:S(2)}, u32[]{:S(2)}) collective-permute-start(bf16[64,2176]{1,0:T(8,128)(2,1)} %get-tuple-element.57), channel_id=1, source_target_pairs={{0,1},{1,0},{2,3},{3,2},{4,5},{5,4},{6,7},{7,6},{8,9},{9,8},{10,11... | collective-permute-start | bytes 835592 | tf_op jit(solution)/shard_map/ppermute | solution.py:439
  411.6 63.6 %collective-permute-start.46 = (bf16[64,2176]{1,0:T(8,128)(2,1)S(1)}, bf16[64,2176]{1,0:T(8,128)(2,1)S(1)}, u32[]{:S(2)}, u32[]{:S(2)}) collective-permute-start(bf16[64,2176]{1,0:T(8,128)(2,1)S(1)} %get-tuple-element.58), channel_id=1, source_target_pairs={{0,8},{1,9},{2,10},{3,11},{4,12},{5,13},{6,14},{7,15},{8,0},{9,1},... | collective-permute-start | bytes 835592 | tf_op jit(solution)/shard_map/ppermute | solution.py:439
  413.7 61.9 %collective-permute-start.47 = (bf16[64,2176]{1,0:T(8,128)(2,1)S(1)}, bf16[64,2176]{1,0:T(8,128)(2,1)S(1)}, u32[]{:S(2)}, u32[]{:S(2)}) collective-permute-start(bf16[64,2176]{1,0:T(8,128)(2,1)S(1)} %get-tuple-element.59), channel_id=1, source_target_pairs={{0,9},{1,8},{2,11},{3,10},{4,13},{5,12},{6,15},{7,14},{8,1},{9,0},... | collective-permute-start | bytes 835592 | tf_op jit(solution)/shard_map/ppermute | solution.py:439
  421.2 57.1 %collective-permute-start.48 = (bf16[64,2176]{1,0:T(8,128)(2,1)S(1)}, bf16[64,2176]{1,0:T(8,128)(2,1)S(1)}, u32[]{:S(2)}, u32[]{:S(2)}) collective-permute-start(bf16[64,2176]{1,0:T(8,128)(2,1)S(1)} %get-tuple-element.60), channel_id=1, source_target_pairs={{0,16},{1,17},{2,18},{3,19},{4,20},{5,21},{6,22},{7,23},{8,24},{9,... | collective-permute-start | bytes 835592 | tf_op jit(solution)/shard_map/ppermute | solution.py:439
  478.3 59.8 %collective-permute-start.28 = (bf16[128,2048]{1,0:T(8,128)(2,1)S(1)}, bf16[128,2048]{1,0:T(8,128)(2,1)S(1)}, u32[]{:S(2)}, u32[]{:S(2)}) collective-permute-start(bf16[128,2048]{1,0:T(8,128)(2,1)S(1)} %get-tuple-element.89), channel_id=1, source_target_pairs={{0,8},{1,9},{2,10},{3,11},{4,12},{5,13},{6,14},{7,15},{8,0},{9,1},... | collective-permute-start | bytes 1572872 | tf_op jit(solution)/shard_map/ppermute | solution.py:439
  478.8 59.2 %collective-permute-start.30 = (bf16[128,2048]{1,0:T(8,128)(2,1)S(1)}, bf16[128,2048]{1,0:T(8,128)(2,1)S(1)}, u32[]{:S(2)}, u32[]{:S(2)}) collective-permute-start(bf16[128,2048]{1,0:T(8,128)(2,1)S(1)} %get-tuple-element.90), channel_id=1, source_target_pairs={{0,24},{1,25},{2,26},{3,27},{4,28},{5,29},{6,30},{7,31},{8,16},{9,... | collective-permute-start | bytes 1572872 | tf_op jit(solution)/shard_map/ppermute | solution.py:439
  484.4 61.3 %collective-permute-start.29 = (bf16[128,2048]{1,0:T(8,128)(2,1)S(1)}, bf16[128,2048]{1,0:T(8,128)(2,1)S(1)}, u32[]{:S(2)}, u32[]{:S(2)}) collective-permute-start(bf16[128,2048]{1,0:T(8,128)(2,1)S(1)} %get-tuple-element.91), channel_id=1, source_target_pairs={{0,16},{1,17},{2,18},{3,19},{4,20},{5,21},{6,22},{7,23},{8,24},{9,... | collective-permute-start | bytes 1572872 | tf_op jit(solution)/shard_map/ppermute | solution.py:439
  505.9 42.6 %collective-permute-start.62 = (f32[320]{0:T(512)S(1)}, f32[320]{0:T(512)S(1)}, u32[]{:S(2)}, u32[]{:S(2)}) collective-permute-start(f32[320]{0:T(512)S(1)} %get-tuple-element.80), channel_id=1, source_target_pairs={{0,8},{1,9},{2,10},{3,11},{4,12},{5,13},{6,14},{7,15},{8,0},{9,1},... | collective-permute-start | bytes 3848 | tf_op jit(solution)/shard_map/ppermute | solution.py:439
  (67 other events, 1699.2 us)
